TPU v7x, 128 devices: a whole 4x4x4 slice. The times are simulated.
128 devices in a mesh: seq: 16 (over x, z), ch: 8 (over y, core).
Axes of the slice: x: 4, y: 4, z: 4, core: 2. Of those that a mesh axis runs over, the one named last changes fastest.
Arguments:
- features: bfloat16 [2048, 8192], P('seq', 'ch'), may hold values from -6 to 6
- qkv_weight: bfloat16 [1664, 3, 8192], P('seq', None, 'ch'), may hold values from -0.0625 to 0.0625
- grad_out: bfloat16 [1664, 2048], P('ch', 'seq'), may hold values from -6 to 6
- residues: float32 [1664, 16], P('ch'), may hold values from -1 to 1
- log_rates: float32 [1664, 16], P('ch'), may hold values from -10 to -1, as said below
- skip_gain: float32 [1664], P('ch'), may hold values from -1 to 1
Outputs:
- weight_grad: float32 [1664, 3, 8192], P('seq', None, 'ch')
- residue_grad: float32 [1664, 16], P('ch')
- rate_grad: float32 [1664, 16], P('ch')
- skip_grad: float32 [1664], P('ch')
Inputs may be any that keep to these rules, and one draw needn't show every extreme that they name: Each channel's decay rates exp(log_rates) lie between about 1 / 2048 and 3 / 20.
All inputs are finite; a program needn't handle non-finite values.
Results may differ from a plain program's by a relative error of at most 0.029.
Values may be sent and summed in bfloat16 or wider, within the bound.
A program may use at most 64 MiB of HBM per device.

v0:
```python
import math

import jax
import jax.numpy as jnp
from jax import lax
from jax.sharding import PartitionSpec as P

TWO_PI = 2.0 * math.pi


def in_blocks(shard, dim, length):
    before, after = (shard.shape[:dim], shard.shape[dim + 1 :])
    return jnp.moveaxis(shard.reshape(*before, length, -1, *after), dim, 0)


def summed_on_arrival(shard, axis, dim):
    tiles = in_blocks(shard, dim, lax.axis_size(axis))
    arrived = lax.all_to_all(tiles, axis, split_axis=0, concat_axis=0, tiled=True)
    return arrived.astype(jnp.float32).sum(axis=0)


def shortened(shard):
    return jax.tree.map(lambda a: a.astype(jnp.bfloat16) if a.dtype == jnp.float32 else a, shard)


def in_order(tiles, dim):
    tiles = jnp.moveaxis(tiles, 0, dim)
    shape = tiles.shape
    return tiles.reshape(*shape[:dim], shape[dim] * shape[dim + 1], *shape[dim + 2 :])


def gather_packed(arrays, axis, dims):
    ravelled = jnp.concatenate([a.reshape(-1) for a in arrays])
    lines, at, outs = (lax.all_gather(ravelled, axis), 0, [])
    for a, dim in zip(arrays, dims):
        tiles = lines[:, at : at + a.size].reshape(-1, *a.shape)
        outs.append(in_order(tiles, dim))
        at += a.size
    return tuple(outs)


def copy_for_each(shard, axis):
    copies = jnp.broadcast_to(shard, (lax.axis_size(axis), *shard.shape))
    return lax.all_to_all(copies, axis, split_axis=0, concat_axis=0, tiled=True)


def gather_directly(shard, axis, dim):
    tiles = copy_for_each(shard, axis)
    return in_order(tiles, dim)


def phase_pair(left_index, right_index, period, sign):
    product = left_index[:, None] * right_index[None, :] % period
    angles = product.astype(jnp.float32) * (TWO_PI / period)
    return (jnp.cos(angles), sign * jnp.sin(angles))


def apply_phases(formula, phases, real_part, imag_part):
    cos_part, sin_part = phases
    if imag_part is None:
        return (jnp.einsum(formula, cos_part, real_part), jnp.einsum(formula, sin_part, real_part))
    real_out = jnp.einsum(formula, cos_part, real_part) - jnp.einsum(formula, sin_part, imag_part)
    imag_out = jnp.einsum(formula, sin_part, real_part) + jnp.einsum(formula, cos_part, imag_part)
    return (real_out, imag_out)


def twist(real_part, imag_part, phases):
    cos_part, sin_part = phases
    return (
        real_part * cos_part - imag_part * sin_part,
        real_part * sin_part + imag_part * cos_part,
    )


def forward_whole(signal):
    row_count, length = signal.shape
    inner_len = 128
    outer_len = 2 * length // inner_len
    blocks = signal.reshape(row_count, outer_len // 2, inner_len)
    outer_index = jnp.arange(outer_len, dtype=jnp.int32)
    half_index = jnp.arange(outer_len // 2, dtype=jnp.int32)
    inner_index = jnp.arange(inner_len, dtype=jnp.int32)
    real_part, imag_part = apply_phases(
        "kn,rnm->rkm", phase_pair(outer_index, half_index, outer_len, -1.0), blocks, None
    )
    real_part, imag_part = twist(
        real_part, imag_part, phase_pair(outer_index, inner_index, 2 * length, -1.0)
    )
    return apply_phases(
        "mj,rkm->rkj", phase_pair(inner_index, inner_index, inner_len, -1.0), real_part, imag_part
    )


def inverse_whole(real_part, imag_part):
    row_count, outer_len, inner_len = real_part.shape
    length = outer_len * inner_len // 2
    outer_index = jnp.arange(outer_len, dtype=jnp.int32)
    half_index = jnp.arange(outer_len // 2, dtype=jnp.int32)
    inner_index = jnp.arange(inner_len, dtype=jnp.int32)
    real_part, imag_part = apply_phases(
        "jm,rkj->rkm", phase_pair(inner_index, inner_index, inner_len, 1.0), real_part, imag_part
    )
    real_part, imag_part = twist(
        real_part, imag_part, phase_pair(outer_index, inner_index, 2 * length, 1.0)
    )
    cos_part, sin_part = phase_pair(half_index, outer_index, outer_len, 1.0)
    real_only = jnp.einsum("nk,rkm->rnm", cos_part, real_part) - jnp.einsum(
        "nk,rkm->rnm", sin_part, imag_part
    )
    return real_only.reshape(row_count, length) / (2.0 * length)


def filter_taps(residues, rates, steps):
    return jnp.sum(
        residues[:, :, None] * jnp.exp(-rates[:, :, None] * steps[None, None, :]), axis=1
    )


def pole_grads(taps_grad, residues, rates, steps):
    decays = jnp.exp(-rates[:, :, None] * steps[None, None, :])
    residue_part = jnp.einsum("ct,crt->cr", taps_grad, decays)
    moment = jnp.einsum("ct,crt->cr", taps_grad * steps[None, :], decays)
    return (residue_part, -residues * rates * moment)


def spectral_products(mixed_re, mixed_im, mid_re, mid_im, taps_re, taps_im):
    conv_re = taps_re * mixed_re - taps_im * mixed_im
    conv_im = taps_re * mixed_im + taps_im * mixed_re
    corr_re = taps_re * mid_re + taps_im * mid_im
    corr_im = taps_re * mid_im - taps_im * mid_re
    grad_re = mixed_re * mid_re + mixed_im * mid_im
    grad_im = mixed_re * mid_im - mixed_im * mid_re
    return (
        jnp.concatenate([conv_re, corr_re, grad_re], 0),
        jnp.concatenate([conv_im, corr_im, grad_im], 0),
    )


def local(features, qkv_weight, grad_out, residues, log_rates, skip_gain):
    block_len = features.shape[0]
    shards = lax.axis_size("seq")
    own_index = lax.axis_index("seq")
    channels = grad_out.shape[0]
    length = block_len * shards
    partial_proj = jnp.einsum(
        "td,cgd->cgt",
        features,
        lax.all_gather(qkv_weight, "seq", axis=0, tiled=True),
        preferred_element_type=jnp.float32,
    )
    projected = summed_on_arrival(partial_proj.astype(jnp.bfloat16), "ch", 0).astype(jnp.bfloat16)
    queries = projected[:, 0].astype(jnp.float32)
    keys = projected[:, 1].astype(jnp.float32)
    values = projected[:, 2].astype(jnp.float32)
    kv_product = keys * values
    grad_upper = grad_out.astype(jnp.float32)
    grad_mid = grad_upper * queries
    rates = jnp.exp(log_rates)
    per_device = channels // shards
    arrived = lax.all_to_all(
        jnp.stack([kv_product, grad_mid]).astype(jnp.bfloat16),
        "seq",
        split_axis=1,
        concat_axis=2,
        tiled=True,
    ).astype(jnp.float32)
    own_residues = lax.dynamic_slice_in_dim(residues, own_index * per_device, per_device, 0)
    own_rates = lax.dynamic_slice_in_dim(rates, own_index * per_device, per_device, 0)
    steps = jnp.arange(length, dtype=jnp.int32).astype(jnp.float32)
    spec_re, spec_im = forward_whole(arrived.reshape(2 * per_device, length))
    taps_re, taps_im = forward_whole(filter_taps(own_residues, own_rates, steps))
    prod_re, prod_im = spectral_products(
        spec_re[:per_device],
        spec_im[:per_device],
        spec_re[per_device:],
        spec_im[per_device:],
        taps_re,
        taps_im,
    )
    restored = inverse_whole(prod_re, prod_im)
    returned = lax.all_to_all(
        shortened(jnp.stack([restored[:per_device], restored[per_device : 2 * per_device]])),
        "seq",
        split_axis=2,
        concat_axis=1,
        tiled=True,
    )
    conv_out = returned[0]
    corr_out = returned[1]
    residue_part, rate_part = pole_grads(restored[2 * per_device :], own_residues, own_rates, steps)
    skip_part = jnp.sum(arrived[0] * arrived[1], axis=1)
    residue_grad, rate_grad, skip_grad = gather_packed(
        (residue_part, rate_part, skip_part), "seq", (0, 0, 0)
    )
    skip_col = skip_gain[:, None]
    grad_query = grad_upper * (conv_out + skip_col * kv_product)
    grad_mix = corr_out + skip_col * grad_mid
    grad_proj = jnp.stack([grad_query, grad_mix * values, grad_mix * keys], axis=1).astype(
        jnp.bfloat16
    )
    full_grad = gather_directly(grad_proj, "ch", 0)
    every_feature = lax.all_gather(features, "seq", axis=0, tiled=True)
    own_rows = lax.all_to_all(full_grad, "seq", split_axis=0, concat_axis=2, tiled=True)

    def add_block(block_index, total):
        grad_piece = lax.dynamic_slice_in_dim(own_rows, block_index * block_len, block_len, 2)
        feature_piece = lax.dynamic_slice_in_dim(
            every_feature, block_index * block_len, block_len, 0
        )
        partial_sum = jnp.einsum(
            "cgt,td->cgd", grad_piece, feature_piece, preferred_element_type=jnp.float32
        )
        rounded = lax.optimization_barrier(partial_sum.astype(jnp.bfloat16))
        return total + rounded.astype(jnp.float32)

    initial = jnp.zeros((own_rows.shape[0], own_rows.shape[1], features.shape[1]), jnp.float32)
    weight_grad = lax.fori_loop(0, shards, add_block, initial)
    return (weight_grad, residue_grad, rate_grad, skip_grad)


def solution(mesh):
    placed = (
        P("seq", "ch"),
        P("seq", None, "ch"),
        P("ch", "seq"),
        P("ch", None),
        P("ch", None),
        P("ch"),
    )
    return jax.shard_map(
        local,
        mesh=mesh,
        in_specs=placed,
        out_specs=(P("seq", None, "ch"), P("ch", None), P("ch", None), P("ch")),
        check_vma=False,
    )
```

profile of v0, /device:TPU:0, one launch (start us, length us, event | category | flops | bytes accessed | tf_op | source)
XLA Modules:
  0.0 325.1 jit_solution(15459386954492270751)
XLA Ops:
  7.2 0.7 all-gather.4.cloned.1.call-update
  8.0 0.7 all-gather.6.cloned.1.call-update
  8.7 0.8 fusion.117
  9.7 0.8 multiply_reduce_fusion
  10.5 81.4 %all-gather.4.cloned.1.call-done = bf16[1664,3,1024]{2,0,1:T(8,128)(2,1)} async-done(((bf16[104,3,1024]{2,0,1:T(8,128)(2,1)}), bf16[1664,3,1024]{2,0,1:T(8,128)(2,1)}) %all-gather.4.cloned.1.call-update) | async-done | bytes 10223632 | tf_op jit(solution)/shard_map/all_gather | solution.py:148
  91.9 6.7 %convolution_convert_fusion.1 = bf16[1664,3,128]{2,0,1:T(8,128)(2,1)S(1)} fusion(bf16[1664,3,1024]{2,0,1:T(8,128)(2,1)} %all-gather.4.cloned.1.call-done, bf16[128,1024]{1,0:T(8,128)(2,1)S(1)} %copy-done.1), kind=kOutput, calls=%fused_computation.6 | convolution fusion | flops 1309261824 | bytes 11763712 | tf_op jit(solution)/shard_map/td,cgd->cgt/dot_general | solution.py:145
  98.6 1.1 copy.90
  99.8 4.3 %all-to-all-start = ((bf16[8,208,3,128]{3,1,2,0:T(8,128)(2,1)}), bf16[8,208,3,128]{3,1,2,0:T(8,128)(2,1)S(1)}, u32[]{:S(2)}, u32[]{:S(2)}) async-start(bf16[8,208,3,128]{3,1,2,0:T(8,128)(2,1)} %copy.90), calls=%async_computation | async-start | bytes 2555904 | tf_op jit(solution)/shard_map/all_to_all | solution.py:18
  106.0 16.5 %all-to-all-done = bf16[8,208,3,128]{3,1,2,0:T(8,128)(2,1)S(1)} async-done(((bf16[8,208,3,128]{3,1,2,0:T(8,128)(2,1)}), bf16[8,208,3,128]{3,1,2,0:T(8,128)(2,1)S(1)}, u32[]{:S(2)}, u32[]{:S(2)}) %all-to-all-start) | async-done | bytes 1277984 | tf_op jit(solution)/shard_map/all_to_all | solution.py:18
  122.7 0.7 copy.91
  123.5 5.3 %all-to-all-start.1 = ((bf16[2,208,128]{2,0,1:T(2,128)(2,1)}), bf16[2,208,128]{2,0,1:T(2,128)(2,1)S(1)}, u32[]{:S(2)}, u32[]{:S(2)}) async-start(bf16[2,208,128]{2,0,1:T(2,128)(2,1)} %copy.91), calls=%async_computation.1 | async-start | bytes 212992 | tf_op jit(solution)/shard_map/all_to_all | solution.py:160
  128.8 8.5 %all-to-all-done.1 = bf16[2,208,128]{2,0,1:T(2,128)(2,1)S(1)} async-done(((bf16[2,208,128]{2,0,1:T(2,128)(2,1)}), bf16[2,208,128]{2,0,1:T(2,128)(2,1)S(1)}, u32[]{:S(2)}, u32[]{:S(2)}) %all-to-all-start.1) | async-done | bytes 106528 | tf_op jit(solution)/shard_map/all_to_all | solution.py:160
  142.5 1.0 fusion.211
  143.6 0.8 copy.94
  144.5 0.8 copy.93
  145.3 2.8 fusion.212
  148.1 1.6 reshape.170
  149.7 11.5 %all_to_all.58 = bf16[16,2,1664]{2,1,0:T(2,128)(2,1)S(1)} all-to-all(bf16[16,2,1664]{2,1,0:T(2,128)(2,1)S(1)} %reshape.170), channel_id=1, replica_groups=mesh['seq'=16,'ch'=8] {'seq'}, dimensions={0} | all-to-all | bytes 212992 | tf_op jit(solution)/shard_map/all_to_all | solution.py:181
  161.2 2.4 reshape.171
  163.6 0.6 copy.109
  164.6 1.2 broadcast_in_dim.5
  165.8 3.8 %all-to-all-start.3 = ((bf16[8,208,3,128]{3,1,2,0:T(8,128)(2,1)}), bf16[8,208,3,128]{3,1,2,0:T(8,128)(2,1)S(1)}, u32[]{:S(2)}, u32[]{:S(2)}) async-start(bf16[8,208,3,128]{3,1,2,0:T(8,128)(2,1)} %broadcast_in_dim.5), calls=%async_computation.3 | async-start | bytes 2555904 | tf_op jit(solution)/shard_map/all_to_all | solution.py:44
  170.9 0.9 slice.91
  172.5 15.2 %all-to-all-done.3 = bf16[8,208,3,128]{3,1,2,0:T(8,128)(2,1)S(1)} async-done(((bf16[8,208,3,128]{3,1,2,0:T(8,128)(2,1)}), bf16[8,208,3,128]{3,1,2,0:T(8,128)(2,1)S(1)}, u32[]{:S(2)}, u32[]{:S(2)}) %all-to-all-start.3) | async-done | bytes 1277984 | tf_op jit(solution)/shard_map/all_to_all | solution.py:44
  187.8 8.9 %copy.99 = bf16[1664,3,128]{2,1,0:T(4,128)(2,1)} copy(bf16[1664,3,128]{2,0,1:T(8,128)(2,1)S(1)} %bitcast.159) | data formatting | bytes 2555904 | tf_op jit(solution)/shard_map/reshape | solution.py:29
  196.7 3.7 %all-to-all-start.4 = ((bf16[1664,3,128]{2,1,0:T(4,128)(2,1)}), bf16[1664,3,128]{2,1,0:T(4,128)(2,1)S(1)}, u32[]{:S(2)}, u32[]{:S(2)}) async-start(bf16[1664,3,128]{2,1,0:T(4,128)(2,1)} %copy.99), calls=%async_computation.4 | async-start | bytes 3407872 | tf_op jit(solution)/shard_map/all_to_all | solution.py:203
  201.8 84.8 %all-reduce = f32[6864]{0:T(1024)S(1)} all-reduce(f32[6864]{0:T(1024)S(1)} %maximum_dynamic-update-slice_fusion), channel_id=2, replica_groups=mesh['seq'=16,'ch'=8] {'seq'}, use_global_device_ids=true, to_apply=%add | all-reduce | flops 6864 | bytes 54912
  286.7 0.7 reshape.144
  287.6 0.7 copy.104
  288.4 0.7 copy.103
  289.6 27.6 %while.14 = (s32[]{:T(128)}, f32[104,3,1024]{2,0,1:T(8,128)S(1)}, bf16[104,3,2048]{2,0,1:T(8,128)(2,1)S(1)}, bf16[2048,1024]{1,0:T(8,128)(2,1)}, s32[]{:T(128)}, /*index=5*/s32[]{:T(128)}, s32[]{:T(128)}, s32[]{:T(128)}) while((s32[]{:T(128)}, f32[104,3,1024]{2,0,1:T(8,128)S(1)}, bf16[104,3,2048]{2,0,1:T(8,128)(2,1)S(1)}, ...), condition=%wide.region_3.4_spmd.clone, body=%wide.region_2.3_spmd.clone.sunk | while | flops 83066888 | bytes 4177045 | solution.py:217
  289.6 1.3 convolution_convert_fusion.3
  291.3 1.3 convolution_convert_fusion.3
  293.1 1.3 convolution_convert_fusion.3
  294.8 1.3 convolution_convert_fusion.3
  296.5 1.3 convolution_convert_fusion.3
  298.3 1.3 convolution_convert_fusion.3
  300.0 1.3 convolution_convert_fusion.3
  301.7 1.3 convolution_convert_fusion.3
  303.4 1.3 convolution_convert_fusion.3
  305.1 1.3 convolution_convert_fusion.3
  306.9 1.3 convolution_convert_fusion.3
  308.6 1.3 convolution_convert_fusion.3
  310.3 1.3 convolution_convert_fusion.3
  312.1 1.3 convolution_convert_fusion.3
  313.8 1.3 convolution_convert_fusion.3
  315.5 1.3 convolution_convert_fusion.3
  317.2 1.0 copy-done
  (96 shorter events, 18.5 us)
Async XLA Ops:
  7.2 84.7 %copy-start.1 = (bf16[128,1024]{1,0:T(8,128)(2,1)S(1)}, bf16[128,1024]{1,0:T(8,128)(2,1)}, u32[]{:S(2)}) copy-start(bf16[128,1024]{1,0:T(8,128)(2,1)} %param.8) | copy-start | bytes 786436
  7.2 84.7 %all-gather.4.cloned.1.call-start = ((), (), s32[]{:S(2)}) async-start(), calls=%async_computation.5 | async-start | bytes 10862592 | tf_op jit(solution)/shard_map/all_gather | solution.py:148
  7.9 281.7 %all-gather.6.cloned.1.call-start = ((), (), s32[]{:S(2)}) async-start(), calls=%async_computation.6 | async-start | bytes 4456448 | tf_op jit(solution)/shard_map/all_gather | solution.py:202
  99.8 22.7 %all-to-all-start = ((bf16[8,208,3,128]{3,1,2,0:T(8,128)(2,1)}), bf16[8,208,3,128]{3,1,2,0:T(8,128)(2,1)S(1)}, u32[]{:S(2)}, u32[]{:S(2)}) async-start(bf16[8,208,3,128]{3,1,2,0:T(8,128)(2,1)} %copy.90), calls=%async_computation | async-start | bytes 2555904 | tf_op jit(solution)/shard_map/all_to_all | solution.py:18
  105.1 17.5 %copy-start.2 = (bf16[208,128]{1,0:T(8,128)(2,1)S(1)}, bf16[208,128]{1,0:T(8,128)(2,1)}, u32[]{:S(2)}) copy-start(bf16[208,128]{1,0:T(8,128)(2,1)} %param.10) | copy-start | bytes 159748
  123.5 13.9 %all-to-all-start.1 = ((bf16[2,208,128]{2,0,1:T(2,128)(2,1)}), bf16[2,208,128]{2,0,1:T(2,128)(2,1)S(1)}, u32[]{:S(2)}, u32[]{:S(2)}) async-start(bf16[2,208,128]{2,0,1:T(2,128)(2,1)} %copy.91), calls=%async_computation.1 | async-start | bytes 212992 | tf_op jit(solution)/shard_map/all_to_all | solution.py:160
  161.2 3.2 copy-start.5
  164.6 5.0 %copy-start.6 = (u32[128]{0:T(128)S(1)}, u32[128]{0:T(128)}, u32[]{:S(2)}) copy-start(u32[128]{0:T(128)} %constant.127) | copy-start | bytes 1540
  165.8 21.9 %all-to-all-start.3 = ((bf16[8,208,3,128]{3,1,2,0:T(8,128)(2,1)}), bf16[8,208,3,128]{3,1,2,0:T(8,128)(2,1)S(1)}, u32[]{:S(2)}, u32[]{:S(2)}) async-start(bf16[8,208,3,128]{3,1,2,0:T(8,128)(2,1)} %broadcast_in_dim.5), calls=%async_computation.3 | async-start | bytes 2555904 | tf_op jit(solution)/shard_map/all_to_all | solution.py:44
  196.7 92.4 %all-to-all-start.4 = ((bf16[1664,3,128]{2,1,0:T(4,128)(2,1)}), bf16[1664,3,128]{2,1,0:T(4,128)(2,1)S(1)}, u32[]{:S(2)}, u32[]{:S(2)}) async-start(bf16[1664,3,128]{2,1,0:T(4,128)(2,1)} %copy.99), calls=%async_computation.4 | async-start | bytes 3407872 | tf_op jit(solution)/shard_map/all_to_all | solution.py:203
  200.4 0.7 copy-start.3
  200.4 0.7 copy-start.4
  317.2 1.0 copy-start
Sparse Core Ops, SparseCore 0:
  10.1 81.7 all-gather.3
  94.0 52.1 all-gather.5
where the time goes:
time: 326 us; the launch traced here: 325 us
  waiting for transfers between devices  123 us (38%)
  blocking collectives  96.2 us (30%)
  matrix products  35.9 us (11%)
  local copies, waits for them, and re-layouts  24.8 us (8%)
  starting transfers between devices  17.1 us (5%)
  between operations  15.2 us (5%)
  other arithmetic  12.4 us (4%)
    unnamed x1, blocking collectives  84.8 us
    all_gather x1, waiting for transfers between devices, local(): lax.all_gather(qkv_weight, 'seq', axis=0, tiled=True)  81.4 us
    dot_general x16, matrix products, add_block(): jnp.einsum('cgt,td->cgd', grad_piece, feature_piece, preferred_element_ty...  20.3 us
    all_to_all x1, waiting for transfers between devices, summed_on_arrival(): lax.all_to_all(tiles, axis, split_axis=0, concat_axis=0, tiled=True)  16.5 us
    all_to_all x1, waiting for transfers between devices, copy_for_each(): return lax.all_to_all(copies, axis, split_axis=0, concat_axis=0, tiled=True)  15.2 us
    all_to_all x1, blocking collectives, local(): lax.all_to_all(shortened(jnp.stack([restored[:per_device], restored[per_d...  11.5 us
    reshape x2, local copies, waits for them, and re-layouts, in_order(): tiles.reshape(*shape[:dim], shape[dim] * shape[dim + 1], *shape[dim + 2:])  9.55 us
    all_to_all x1, waiting for transfers between devices, local(): lax.all_to_all(jnp.stack([kv_product, grad_mid]).astype(jnp.bfloat16), 's...  8.52 us
  transfers between devices with their start and end apart: 6, of which 4 were waited for; matrix products, arithmetic and copies ran while one was open for 14% of the time, Pallas kernels for 0%

commit v1 on v0

v1 whole, which is shorter than its diff:
```python
import jax
import jax.numpy as jnp
from jax import lax
from jax.sharding import PartitionSpec as P

CHUNK = 128


def decays_of(rates, lags):
    return jnp.exp(-rates[:, :, None] * lags[None, None, :])


def toeplitz(taps):
    rows = jnp.arange(CHUNK)
    lag = rows[None, :] - rows[:, None]
    picked = jnp.take(taps, jnp.maximum(lag, 0).reshape(-1), axis=1).reshape(-1, CHUNK, CHUNK)
    return jnp.where(lag[None] >= 0, picked, 0.0)


def diagonal_sums(product):
    padded = jnp.pad(product, ((0, 0), (0, 0), (0, CHUNK)))
    flat = padded.reshape(product.shape[0], -1)[:, : CHUNK * (2 * CHUNK - 1)]
    skewed = flat.reshape(-1, CHUNK, 2 * CHUNK - 1)
    return skewed.sum(axis=1)


def mix(projected, grads, residues, log_rates, gain):
    count = projected.shape[0]
    chunks = projected.shape[2] // CHUNK
    parts = projected.astype(jnp.float32).reshape(count, 3, chunks, CHUNK)
    queries, keys, values = parts[:, 0], parts[:, 1], parts[:, 2]
    grad_upper = grads.astype(jnp.float32).reshape(count, chunks, CHUNK)
    kv = keys * values
    gm = grad_upper * queries
    rates = jnp.exp(log_rates)
    lags = jnp.arange(CHUNK, dtype=jnp.float32)
    near = decays_of(rates, lags)
    far = decays_of(rates, CHUNK - lags)
    taps = (residues[:, :, None] * near).sum(axis=1)
    band = toeplitz(taps)
    conv = jnp.einsum("ckb,cba->cka", kv, band)
    corr = jnp.einsum("cka,cba->ckb", gm, band)
    tails = jnp.einsum("ckb,crb->kcr", kv, far)
    tails_lag = jnp.einsum("ckb,crb->kcr", kv, far * (CHUNK - lags))
    heads = jnp.einsum("cka,cra->kcr", gm, near)
    heads_lag = jnp.einsum("cka,cra->kcr", gm, near * lags)
    step = jnp.exp(-CHUNK * rates)
    state = jnp.zeros_like(step)
    state_lag = jnp.zeros_like(step)
    states, states_lag = [], []
    for k in range(chunks):
        states.append(state)
        states_lag.append(state_lag)
        state_lag = step * (state_lag + CHUNK * state) + tails_lag[k]
        state = step * state + tails[k]
    adjoint = jnp.zeros_like(step)
    adjoints = []
    for k in reversed(range(chunks)):
        adjoints.append(adjoint)
        adjoint = step * adjoint + heads[k]
    states = jnp.stack(states)
    states_lag = jnp.stack(states_lag)
    adjoints = jnp.stack(adjoints[::-1])
    conv = conv + jnp.einsum("kcr,cra->cka", states * residues, near)
    corr = corr + jnp.einsum("kcr,crb->ckb", adjoints * residues, far)
    product = jnp.einsum("cka,ckb->cba", gm, kv)
    rolled = jnp.where((lags[None, :] >= lags[:, None])[None], product, 0.0)
    sums = diagonal_sums(rolled[:, ::-1])[:, CHUNK - 1 :]
    residue_grad = jnp.einsum("cj,crj->cr", sums, near, precision="highest") + (heads * states).sum(0)
    moment = jnp.einsum("cj,crj->cr", sums * lags, near, precision="highest") + (
        heads_lag * states + heads * states_lag
    ).sum(0)
    rate_grad = -residues * rates * moment
    skip_grad = (gm * kv).sum((1, 2))
    col = gain[:, None, None]
    grad_query = grad_upper * (conv + col * kv)
    grad_mix = corr + col * gm
    grad_proj = jnp.stack([grad_query, grad_mix * values, grad_mix * keys], axis=1)
    grad_proj = grad_proj.astype(jnp.bfloat16).reshape(count, 3, -1)
    return grad_proj, residue_grad, rate_grad, skip_grad


def local(features, qkv_weight, grad_out, residues, log_rates, skip_gain):
    seq = lax.axis_index("seq")
    ch = lax.axis_index("ch")
    ways = lax.axis_size("ch")
    every = lax.all_gather(features, "seq", axis=0, tiled=True)
    per = qkv_weight.shape[0] // ways

    def to_owner(rows):
        halves = rows.reshape(2, ways, per, *rows.shape[1:])
        picked = lax.dynamic_index_in_dim(halves, seq % 2, 0, keepdims=False)
        arrived = lax.all_to_all(picked, "ch", split_axis=0, concat_axis=0, tiled=True)
        return lax.dynamic_index_in_dim(arrived, seq // 2, 0, keepdims=False)

    grads = to_owner(lax.all_gather(grad_out, "seq", axis=1, tiled=True))
    packed = to_owner(jnp.concatenate([residues, log_rates, skip_gain[:, None]], axis=1))
    order = residues.shape[1]
    partial = jnp.einsum("cgd,td->cgt", qkv_weight, every, preferred_element_type=jnp.float32)
    tiles = partial.astype(jnp.bfloat16).reshape(ways, per, *partial.shape[1:])
    arrived = lax.all_to_all(tiles, "ch", split_axis=0, concat_axis=0, tiled=True)
    projected = arrived.astype(jnp.float32).sum(axis=0).astype(jnp.bfloat16)
    grad_proj, residue_grad, rate_grad, skip_grad = mix(
        projected, grads, packed[:, :order], packed[:, order : 2 * order], packed[:, 2 * order]
    )
    full = lax.all_gather(grad_proj, "ch", axis=0, tiled=True)
    weight_grad = jnp.einsum("cgt,td->cgd", full, every, preferred_element_type=jnp.float32)
    small = jnp.concatenate([residue_grad, rate_grad, skip_grad[:, None]], axis=1)
    gathered = lax.all_gather(small, ("seq", "ch"), axis=0, tiled=True)
    block = residues.shape[0]
    own = lax.dynamic_slice_in_dim(gathered, ch * block, block, 0)
    return weight_grad, own[:, :order], own[:, order : 2 * order], own[:, 2 * order]


def solution(mesh):
    placed = (
        P("seq", "ch"),
        P("seq", None, "ch"),
        P("ch", "seq"),
        P("ch", None),
        P("ch", None),
        P("ch"),
    )
    return jax.shard_map(
        local,
        mesh=mesh,
        in_specs=placed,
        out_specs=(P("seq", None, "ch"), P("ch", None), P("ch", None), P("ch")),
        check_vma=False,
    )
```

time: 326 us -> 244 us (0.75)
  the two profiles are of different devices: /device:TPU:0 before, /device:TPU:1 now
where the time goes in v1:
time: 244 us; the launch traced here: 243 us
  local copies, waits for them, and re-layouts  83.2 us (34%)
  blocking collectives  60.4 us (25%)
  waiting for transfers between devices  29.8 us (12%)
  other arithmetic  22.4 us (9%)
  starting transfers between devices  19.2 us (8%)
  between operations  14.5 us (6%)
  matrix products  13.6 us (6%)
    gather x2, local copies, waits for them, and re-layouts, toeplitz(): jnp.take(taps, jnp.maximum(lag, 0).reshape(-1), axis=1)  61.2 us
    all_gather x1, blocking collectives, local(): gathered = lax.all_gather(small, ('seq', 'ch'), axis=0, tiled=True)  35.8 us
    all_gather x1, blocking collectives, local(): grads = to_owner(lax.all_gather(grad_out, 'seq', axis=1, tiled=True))  24.6 us
    all_to_all x1, waiting for transfers between devices, local(): lax.all_to_all(tiles, 'ch', split_axis=0, concat_axis=0, tiled=True)  16.3 us
    all_to_all x2, starting transfers between devices, to_owner(): lax.all_to_all(picked, 'ch', split_axis=0, concat_axis=0, tiled=True)  14 us
    all_gather x1, waiting for transfers between devices, local(): every = lax.all_gather(features, 'seq', axis=0, tiled=True)  12.8 us
    unnamed x17, other arithmetic  11.9 us
    unnamed x42, local copies, waits for them, and re-layouts  8.52 us
  transfers between devices with their start and end apart: 5, of which 2 were waited for; matrix products, arithmetic and copies ran while one was open for 8% of the time, Pallas kernels for 0%

profile of v1, /device:TPU:1, one launch (start us, length us, event | category | flops | bytes accessed | tf_op | source)
XLA Modules:
  0.0 243.0 jit_solution(13109513749314422481)
XLA Ops:
  7.2 0.7 all-gather.4.cloned.1.call-update
  7.9 0.8 concatenate.17
  8.9 0.8 concatenate.15
  9.9 0.8 concatenate.16
  11.1 0.7 reshape.142
  11.8 6.0 %all-to-all-start.2 = ((f32[8,1,429]{2,1,0:T(1,128)}), f32[8,1,429]{2,1,0:T(1,128)S(1)}, u32[]{:S(2)}, u32[]{:S(2)}) async-start(f32[8,1,429]{2,1,0:T(1,128)} %reshape.142), calls=%async_computation.2 | async-start | bytes 32768 | tf_op jit(solution)/shard_map/all_to_all | solution.py:93
  17.8 24.6 %all_gather.12 = bf16[208,2048]{1,0:T(8,128)(2,1)S(1)} all-gather(bf16[208,128]{1,0:T(8,128)(2,1)} %param.8), channel_id=1, replica_groups=mesh['seq'=16,'ch'=8] {'seq'}, dimensions={1}, use_global_device_ids=true | all-gather | bytes 905216 | tf_op jit(solution)/shard_map/all_gather | solution.py:96
  43.2 0.8 dynamic-slice_bitcast_fusion
  44.7 8.1 %all-to-all-start = ((bf16[8,13,2048]{2,1,0:T(8,128)(2,1)}), bf16[8,13,2048]{2,1,0:T(8,128)(2,1)}, u32[]{:S(2)}, u32[]{:S(2)}) async-start(bf16[8,13,2048]{2,1,0:T(8,128)(2,1)} %dynamic-slice_bitcast_fusion), calls=%async_computation | async-start | bytes 1048576 | tf_op jit(solution)/shard_map/all_to_all | solution.py:93
  52.8 12.8 %all-gather.4.cloned.1.call-done = bf16[2048,1024]{1,0:T(8,128)(2,1)} async-done(((bf16[128,1024]{1,0:T(8,128)(2,1)}), bf16[2048,1024]{1,0:T(8,128)(2,1)}) %all-gather.4.cloned.1.call-update) | async-done | bytes 4194320 | tf_op jit(solution)/shard_map/all_gather | solution.py:87
  65.5 3.7 %fusion.4 = bf16[104,3,2048]{2,0,1:T(8,128)(2,1)S(1)} fusion(bf16[104,3,1024]{2,0,1:T(8,128)(2,1)S(1)} %copy-done, bf16[2048,1024]{1,0:T(8,128)(2,1)} %all-gather.4.cloned.1.call-done), kind=kOutput, calls=%fused_computation.5 | convolution fusion | flops 1309261824 | bytes 6111232 | tf_op jit(solution)/shard_map/cgd,td->cgt/dot_general | solution.py:99
  69.7 1.3 copy.112
  71.0 5.1 %all-to-all-start.1 = ((bf16[8,13,3,2048]{3,1,2,0:T(8,128)(2,1)}), bf16[8,13,3,2048]{3,1,2,0:T(8,128)(2,1)S(1)}, u32[]{:S(2)}, u32[]{:S(2)}) async-start(bf16[8,13,3,2048]{3,1,2,0:T(8,128)(2,1)} %copy.112), calls=%async_computation.1 | async-start | bytes 3145728 | tf_op jit(solution)/shard_map/all_to_all | solution.py:101
  77.9 0.7 reduce.5
  78.7 0.7 slice_reduce_fusion
  79.5 0.9 dynamic-slice_convert_fusion
  80.4 16.3 %all-to-all-done.1 = bf16[8,13,3,2048]{3,1,2,0:T(8,128)(2,1)S(1)} async-done(((bf16[8,13,3,2048]{3,1,2,0:T(8,128)(2,1)}), bf16[8,13,3,2048]{3,1,2,0:T(8,128)(2,1)S(1)}, u32[]{:S(2)}, u32[]{:S(2)}) %all-to-all-start.1) | async-done | bytes 1277984 | tf_op jit(solution)/shard_map/all_to_all | solution.py:101
  97.1 0.7 multiply_reduce_fusion.1
  98.5 0.9 fusion.29
  99.6 0.7 constant_dynamic-update-slice_fusion.31
  100.3 0.7 constant_dynamic-update-slice_fusion.45
  101.0 0.7 constant_dynamic-update-slice_fusion.44
  101.7 0.7 constant_dynamic-update-slice_fusion.43
  102.4 0.7 constant_dynamic-update-slice_fusion.42
  103.1 0.7 constant_dynamic-update-slice_fusion.41
  103.8 0.7 constant_dynamic-update-slice_fusion.40
  104.5 0.7 constant_dynamic-update-slice_fusion.39
  105.2 0.7 constant_dynamic-update-slice_fusion.38
  105.9 0.7 constant_dynamic-update-slice_fusion.37
  107.2 0.7 constant_dynamic-update-slice_fusion.36
  108.4 0.7 constant_dynamic-update-slice_fusion.35
  109.7 0.7 constant_dynamic-update-slice_fusion.34
  111.6 0.7 constant_dynamic-update-slice_fusion.2
  114.0 1.2 copy.166
  115.3 3.8 %reshape.121 = f32[13,128,255]{2,1,0:T(8,128)} reshape(f32[13,32640]{1,0:T(8,128)S(1)} %slice.262) | data formatting | bytes 3394560 | tf_op jit(solution)/shard_map/reshape | solution.py:23
  119.1 1.6 reduce_sum.59
  121.2 1.4 constant_dynamic-update-slice_fusion.33
  122.6 1.4 constant_dynamic-update-slice_fusion.32
  124.0 1.1 multiply_reduce_fusion
  125.4 57.4 %gather_fusion = bf16[16384,13]{1,0:T(8,128)(2,1)} fusion(bf16[13,128]{0,1:T(8,128)(2,1)S(1)} %copy.117, s32[16384]{0:T(1024)S(1)} %copy-done.6), kind=kCustom, calls=%fused_computation | custom fusion | bytes 917504 | tf_op jit(solution)/shard_map/jit(_take)/gather | solution.py:16
  182.8 3.8 %copy.149 = bf16[13,128,128]{2,1,0:T(8,128)(2,1)S(1)} copy(bf16[13,128,128]{0,2,1:T(8,128)(2,1)} %bitcast.593) | data formatting | bytes 851968 | tf_op jit(solution)/shard_map/jit(_take)/gather | solution.py:16
  187.3 0.7 constant_dynamic-update-slice_fusion.17
  188.6 0.9 broadcast_multiply_fusion.1
  190.1 1.1 pad_maximum_fusion
  191.8 35.8 %all-gather = f32[128,13,33]{2,1,0:T(8,128)S(1)} all-gather(f32[1,13,33]{2,1,0:T(8,128)S(1)} %maximum_bitcast_fusion), channel_id=1, replica_groups=mesh['seq'=16,'ch'=8] {'seq','ch'}, dimensions={0}, use_global_device_ids=true | all-gather | bytes 221364 | tf_op jit(solution)/shard_map/all_gather | solution.py:109
  227.8 0.7 copy.144
  229.1 0.7 dynamic-slice_reduce_fusion
  229.9 6.2 %fusion = f32[104,3,1024]{2,0,1:T(8,128)} fusion(bf16[2048,1024]{1,0:T(8,128)(2,1)} %all-gather.4.cloned.1.call-done, bf16[104,3,2048]{2,1,0:T(4,128)(2,1)} %all-gather.6.cloned.1.call-done), kind=kOutput, calls=%fused_computation.1 | convolution fusion | flops 1308622848 | bytes 6750208 | tf_op jit(solution)/shard_map/cgt,td->cgd/dot_general | solution.py:107
  (88 shorter events, 14.6 us)
Async XLA Ops:
  7.2 58.4 %copy-start = (bf16[104,3,1024]{2,0,1:T(8,128)(2,1)S(1)}, bf16[104,3,1024]{2,0,1:T(8,128)(2,1)}, u32[]{:S(2)}) copy-start(bf16[104,3,1024]{2,0,1:T(8,128)(2,1)} %param.7) | copy-start | bytes 1916932
  7.2 58.3 %all-gather.4.cloned.1.call-start = ((), (), s32[]{:S(2)}) async-start(), calls=%async_computation.3 | async-start | bytes 4456448 | tf_op jit(solution)/shard_map/all_gather | solution.py:87
  11.8 32.9 %all-to-all-start.2 = ((f32[8,1,429]{2,1,0:T(1,128)}), f32[8,1,429]{2,1,0:T(1,128)S(1)}, u32[]{:S(2)}, u32[]{:S(2)}) async-start(f32[8,1,429]{2,1,0:T(1,128)} %reshape.142), calls=%async_computation.2 | async-start | bytes 32768 | tf_op jit(solution)/shard_map/all_to_all | solution.py:93
  44.7 26.3 %all-to-all-start = ((bf16[8,13,2048]{2,1,0:T(8,128)(2,1)}), bf16[8,13,2048]{2,1,0:T(8,128)(2,1)}, u32[]{:S(2)}, u32[]{:S(2)}) async-start(bf16[8,13,2048]{2,1,0:T(8,128)(2,1)} %dynamic-slice_bitcast_fusion), calls=%async_computation | async-start | bytes 1048576 | tf_op jit(solution)/shard_map/all_to_all | solution.py:93
  71.0 25.7 %all-to-all-start.1 = ((bf16[8,13,3,2048]{3,1,2,0:T(8,128)(2,1)}), bf16[8,13,3,2048]{3,1,2,0:T(8,128)(2,1)S(1)}, u32[]{:S(2)}, u32[]{:S(2)}) async-start(bf16[8,13,3,2048]{3,1,2,0:T(8,128)(2,1)} %copy.112), calls=%async_computation.1 | async-start | bytes 3145728 | tf_op jit(solution)/shard_map/all_to_all | solution.py:101
  76.1 153.8 %all-gather.6.cloned.1.call-start = ((), (), s32[]{:S(2)}) async-start(), calls=%async_computation.4 | async-start | bytes 1916928 | tf_op jit(solution)/shard_map/all_gather | solution.py:106
  76.1 22.4 %copy-start.9 = (f32[128]{0:T(128)}, f32[128]{0:T(128)S(1)}, u32[]{:S(2)}) copy-start(f32[128]{0:T(128)S(1)} %iota_subtract_fusion.1) | copy-start | bytes 1540
  80.4 19.2 %copy-start.1 = (f32[2,8,16,128]{3,2,1,0:T(8,128)}, f32[2,8,16,128]{3,2,1,0:T(8,128)S(1)}, u32[]{:S(2)}) copy-start(f32[2,8,16,128]{3,2,1,0:T(8,128)S(1)} %copy.165) | copy-start | bytes 393220
  99.6 12.8 %copy-start.3 = (f32[16,13,16]{2,1,0:T(8,128)}, f32[16,13,16]{2,1,0:T(8,128)S(1)}, u32[]{:S(2)}) copy-start(f32[16,13,16]{2,1,0:T(8,128)S(1)} %get-tuple-element.103) | copy-start | bytes 39940
  119.1 4.9 %copy-start.5 = (f32[13,16,16]{1,2,0:T(8,128)S(1)}, f32[13,16,16]{1,2,0:T(8,128)}, u32[]{:S(2)}) copy-start(f32[13,16,16]{1,2,0:T(8,128)} %fusion.29) | copy-start | bytes 39940
  119.1 6.3 %copy-start.6 = (s32[16384]{0:T(1024)S(1)}, s32[16384]{0:T(1024)}, u32[]{:S(2)}) copy-start(s32[16384]{0:T(1024)} %bitcast_clamp_fusion) | copy-start | bytes 196612
  182.8 3.9 %copy-start.7 = (pred[128,128]{1,0:T(8,128)(4,1)S(1)}, pred[128,128]{1,0:T(8,128)(4,1)}, u32[]{:S(2)}) copy-start(pred[128,128]{1,0:T(8,128)(4,1)} %get-tuple-element.105) | copy-start | bytes 49156
  182.8 3.9 %copy-start.8 = (pred[128,128]{1,0:T(8,128)(4,1)S(1)}, pred[128,128]{1,0:T(8,128)(4,1)}, u32[]{:S(2)}) copy-start(pred[128,128]{1,0:T(8,128)(4,1)} %get-tuple-element.106) | copy-start | bytes 49156
  186.6 2.0 copy-start.4
  186.6 2.9 %copy-start.10 = (f32[128]{0:T(128)S(1)}, f32[128]{0:T(128)}, u32[]{:S(2)}) copy-start(f32[128]{0:T(128)} %copy-done.9) | copy-start | bytes 1540
  186.6 2.9 %copy-start.11 = (f32[13]{0:T(128)S(1)}, f32[13]{0:T(128)}, u32[]{:S(2)}) copy-start(f32[13]{0:T(128)} %slice_reduce_fusion) | copy-start | bytes 160
  186.7 3.2 %copy-start.2 = (f32[2,8,16,128]{3,2,1,0:T(8,128)S(1)}, f32[2,8,16,128]{3,2,1,0:T(8,128)}, u32[]{:S(2)}) copy-start(f32[2,8,16,128]{3,2,1,0:T(8,128)} %copy-done.1) | copy-start | bytes 393220
  187.0 4.2 %copy-start.12 = (f32[13]{0:T(128)S(1)}, f32[13]{0:T(128)}, u32[]{:S(2)}) copy-start(f32[13]{0:T(128)} %get-tuple-element.40) | copy-start | bytes 160
Sparse Core Ops, SparseCore 0:
  10.1 55.3 all-gather.3
  191.3 23.0 all-gather.5

commit v2 on v1

v2 whole, which is shorter than its diff:
```python
import functools

import jax
import jax.numpy as jnp
from jax import lax
from jax.experimental import pallas as pl
from jax.experimental.pallas import tpu as pltpu
from jax.sharding import PartitionSpec as P

F32, BF16 = jnp.float32, jnp.bfloat16
CHUNK = 128
SIDE = 4
SHARDS = SIDE * SIDE
WAYS = 2 * SIDE
ROWS = 16
TRIO = 3 * ROWS
STATE = 16
MESH = pl.DeviceIdType.MESH
PARAM_ROWS = 5 * ROWS

NT = (((1,), (1,)), ((), ()))
TN = (((0,), (0,)), ((), ()))
NN = (((1,), (0,)), ((), ()))


def mul(a, b, dims=NN):
    return lax.dot_general(a, b, dims, preferred_element_type=F32)


def iota(shape, dim):
    return lax.broadcasted_iota(jnp.int32, shape, dim)


def sum_partials(parts, grads, kvs, gms, grs, proj):
    flip = (iota((CHUNK, CHUNK), 0) + iota((CHUNK, CHUNK), 1) == CHUNK - 1).astype(BF16)

    def body(k, skip):
        total = parts[0, k].astype(F32)
        for way in range(1, WAYS):
            total = total + parts[way, k].astype(F32)
        rounded = total.astype(BF16)
        proj[k] = rounded
        wide = rounded.astype(F32)
        kv = wide[ROWS : 2 * ROWS] * wide[2 * ROWS :]
        gm = grads[k].astype(F32) * wide[:ROWS]
        kvs[k] = kv
        gms[k] = gm
        grs[k] = mul(gm.astype(BF16), flip)
        return skip + kv * gm

    return lax.fori_loop(0, SHARDS, body, jnp.zeros((ROWS, CHUNK), F32), unroll=4)


def carry(values, step, lagged, reverse):
    row = iota(values.shape, 0)
    shape = values.shape
    decay = jnp.broadcast_to(step, shape)
    reach = 1
    while reach < shape[0]:
        amount = shape[0] - reach if reverse else reach
        keep = row < shape[0] - reach if reverse else row >= reach
        near = jnp.where(keep, decay * pltpu.roll(values, amount, 0), 0.0)
        if lagged is not None:
            moved = jnp.where(keep, decay * pltpu.roll(lagged, amount, 0), 0.0)
            lagged = lagged + moved + (CHUNK * reach) * near
        values = values + near
        decay = decay * decay
        reach *= 2
    return values, lagged


def before(values, reverse):
    row = iota(values.shape, 0)
    last = values.shape[0] - 1
    if reverse:
        return jnp.where(row < last, pltpu.roll(values, last, 0), 0.0)
    return jnp.where(row >= 1, pltpu.roll(values, 1, 0), 0.0)


def mix_channel(c, params, kvs, gms, grs, convs, corrs, small):
    lane = iota((STATE, CHUNK), 1).astype(F32)
    rates = jnp.exp(params[0:STATE, c : c + 1])
    residues = params[STATE : 2 * STATE, c : c + 1]
    near = jnp.exp(-rates * lane)
    far = jnp.exp(-rates * (CHUNK - lane))
    taps = jnp.sum(residues * near, axis=0, keepdims=True)
    upper = iota((CHUNK, CHUNK), 1) >= iota((CHUNK, CHUNK), 0)
    spread = pltpu.roll(jnp.broadcast_to(taps, (CHUNK, CHUNK)), 0, 1, stride=1, stride_axis=0)
    band = jnp.where(upper, spread, 0.0).astype(BF16)
    kv = kvs[:, c, :].astype(BF16)
    gm = gms[:, c, :].astype(BF16)
    gr = grs[:, c, :].astype(BF16)
    near_b, far_b = near.astype(BF16), far.astype(BF16)
    near_lag = (near * lane).astype(BF16)
    far_lag = (far * (CHUNK - lane)).astype(BF16)
    tails = mul(kv, jnp.concatenate([far_b, far_b, far_b], 0), NT)
    tails_lag = mul(kv, jnp.concatenate([far_lag, far_lag, far_lag], 0), NT)
    heads = mul(gm, jnp.concatenate([near_b, near_lag, near_b], 0), NT)
    row_rates = jnp.exp(params[2 * STATE + c : 2 * STATE + c + 1, 0 : 3 * STATE])
    step = jnp.exp(-CHUNK * row_rates)
    row_residues = params[3 * STATE + c : 3 * STATE + c + 1, 0:STATE]
    states, states_lag = carry(tails, step, tails_lag, False)
    states, states_lag = before(states, False), before(states_lag, False)
    third = iota(states.shape, 1) < 2 * STATE
    inter = jnp.sum(heads * jnp.where(third, states, states_lag), axis=0, keepdims=True)
    adjoints, _ = carry(heads[:, 0:STATE], step[:, 0:STATE], None, True)
    adjoints = before(adjoints, True)
    conv = mul(kv, band) + mul((states[:, 0:STATE] * row_residues).astype(BF16), near_b)
    corr = mul(gm, band, NT) + mul((adjoints * row_residues).astype(BF16), far_b)
    convs[:, c, :] = conv
    corrs[:, c, :] = corr
    product = mul(kv, gr, TN)
    skewed = jnp.where(upper, pltpu.roll(product, 0, 1, stride=1, stride_axis=0), 0.0)
    sums = jnp.sum(skewed, axis=0, keepdims=True)
    back = far * jnp.exp(rates)
    weights = jnp.concatenate([back, back * (CHUNK - 1 - lane), jnp.zeros_like(back)], 0)
    wide = jnp.broadcast_to(sums, (ROWS, CHUNK)).astype(BF16)
    intra = mul(wide, weights.astype(BF16), NT)[0:1]
    small[c : c + 1, 0 : 3 * STATE] = inter + intra


def grads_of(params, grads, proj, kvs, gms, convs, corrs, mine):
    gain = params[4 * ROWS :, :]

    def body(k, _):
        wide = proj[k].astype(F32)
        keys, values = wide[ROWS : 2 * ROWS], wide[2 * ROWS :]
        grad_mix = corrs[k] + gain * gms[k]
        query = grads[k].astype(F32) * (convs[k] + gain * kvs[k])
        lanes = pl.ds(pl.multiple_of(k * CHUNK, CHUNK), CHUNK)
        mine[0:ROWS, lanes] = query.astype(BF16)
        mine[ROWS : 2 * ROWS, lanes] = (grad_mix * values).astype(BF16)
        mine[2 * ROWS :, lanes] = (grad_mix * keys).astype(BF16)
        return 0

    lax.fori_loop(0, SHARDS, body, 0, unroll=4)


def mix(count, params, parts, grads, kvs, gms, grs, proj, convs, corrs, small, mine):
    skip = sum_partials(parts, grads, kvs, gms, grs, proj)
    convs[...] = jnp.zeros_like(convs)
    corrs[...] = jnp.zeros_like(corrs)
    small[...] = jnp.zeros_like(small)
    for c in range(count):
        mix_channel(c, params, kvs, gms, grs, convs, corrs, small)
    lane = iota((ROWS, CHUNK), 1)
    summed = jnp.sum(skip, axis=1, keepdims=True)
    small[...] = jnp.where(lane == 3 * STATE, summed, small[...])
    grads_of(params, grads, proj, kvs, gms, convs, corrs, mine)


def kernel(
    count, feat, weight, gout, pars, wgrad, shared,
    every, wbuf, partial, parts, grads, params, kvs, gms, grs, proj, convs, corrs, small, full,
    local_sem, f_send, f_recv, r_send, r_recv, g_send, g_recv, p_send, p_recv, a_send, a_recv,
    s_send, s_recv,
):
    seq, ch = lax.axis_index("seq"), lax.axis_index("ch")
    x, z = seq // SIDE, seq % SIDE
    y, core = ch // 2, ch % 2
    home = seq // 2
    at_home = ch == home

    feat_in = pltpu.make_async_copy(feat, every.at[seq], local_sem.at[0])
    weight_in = pltpu.make_async_copy(weight, wbuf, local_sem.at[1])
    feat_in.start()
    weight_in.start()

    def ring(value, step):
        return (value + step + SIDE) % SIDE

    def place(v, p, q):
        return p * SIDE + q if v == 0 else q * SIDE + p

    def spot(v):
        return (x, z) if v == 0 else (z, x)

    barrier = pltpu.get_barrier_semaphore()

    def greet(s, c):
        pl.semaphore_signal(barrier, inc=1, device_id={"seq": s, "ch": c}, device_id_type=MESH)

    for v in range(2):
        p, q = spot(v)
        for step in (-1, 1):
            greet(place(v, ring(p, step), q), ch)
    for i in range(1, WAYS):
        greet(seq, (ch + i) % WAYS)

    def greet_far(i, _):
        @pl.when(jnp.logical_not(jnp.logical_and(i == seq, at_home)))
        def _():
            greet(i, home)

        @pl.when(jnp.logical_not(jnp.logical_and(2 * ch + i // WAYS == seq, i % WAYS == ch)))
        def _():
            greet(2 * ch + i // WAYS, i % WAYS)

        return 0

    lax.fori_loop(0, SHARDS, greet_far, 0)

    @pl.when(at_home)
    def _():
        pl.semaphore_wait(barrier, 4 + (WAYS - 1) + 2 * (SHARDS - 1))

    @pl.when(jnp.logical_not(at_home))
    def _():
        pl.semaphore_wait(barrier, 4 + (WAYS - 1) + 2 * SHARDS)

    half, quarter = CHUNK // 2, CHUNK // 4
    offs = (0, -1, 1, 2)

    def piece(v, part):
        start = v * half + (quarter if part == "b" else 0)
        return pl.ds(start, half if part == "h" else quarter)

    names = [("P1+", "h"), ("P1-", "h"), ("P2+", "a"), ("P2-", "b")]
    for j in range(3):
        names += [(f"Q1+{j}", "h"), (f"Q1-{j}", "h"), (f"Q2+{j}", "a"), (f"Q2-{j}", "b")]
    names += [("Q1+3a", "a"), ("Q1+3b", "b"), ("Q1-3a", "a"), ("Q1-3b", "b")]
    names += [("Q2+3", "a"), ("Q2-3", "b")]
    number = {name: n for n, (name, _) in enumerate(names)}
    piece_of = dict(names)

    def feature_copy(v, name, arriving):
        p, q = spot(v)
        step = 1 if name[2] == "+" else -1
        hops = int(name[1]) - 1 + (1 if arriving else 0)
        if name[0] == "P":
            source = place(v, ring(p, -step * hops), q)
            target = place(v, ring(p, step), q)
        else:
            source = place(v, ring(p, offs[int(name[3])]), ring(q, -step * hops))
            target = place(v, p, ring(q, step))
        rows = piece(v, piece_of[name])
        return pltpu.make_async_remote_copy(
            src_ref=every.at[source, rows],
            dst_ref=every.at[source, rows],
            send_sem=f_send.at[v, number[name]],
            recv_sem=f_recv.at[v, number[name]],
            device_id={"seq": target},
            device_id_type=MESH,
        )

    def send(v, name):
        feature_copy(v, name, False).start()

    def arrive(v, name):
        feature_copy(v, name, True).wait_recv()

    def owner_copy(shard, i):
        target = (ch + i) % WAYS
        return pltpu.make_async_remote_copy(
            src_ref=partial.at[shard, target],
            dst_ref=parts.at[i, shard],
            send_sem=r_send.at[i],
            recv_sem=r_recv.at[i],
            device_id={"ch": target},
            device_id_type=MESH,
        )

    def project(dx, dz):
        shard = ring(x, dx) * SIDE + ring(z, dz)
        out = mul(wbuf[...], every[shard], NT).astype(BF16).reshape(WAYS, TRIO, CHUNK)
        partial[shard] = out
        parts[0, shard] = partial[shard, ch]
        return shard

    def deliver(shard):
        for i in range(1, WAYS):
            owner_copy(shard, i).start()

    feat_in.wait()
    for v in range(2):
        send(v, "P1+")
        send(v, "P1-")
    for v in range(2):
        send(v, "Q1+0")
        send(v, "Q1-0")

    def grad_copy(i):
        return pltpu.make_async_remote_copy(
            src_ref=gout.at[i],
            dst_ref=grads.at[seq],
            send_sem=g_send.at[i],
            recv_sem=g_recv,
            device_id={"seq": 2 * ch + i // WAYS, "ch": i % WAYS},
            device_id_type=MESH,
        )

    def is_self(i):
        return jnp.logical_and(2 * ch + i // WAYS == seq, i % WAYS == ch)

    def start_grads(i, _):
        @pl.when(is_self(i))
        def _():
            pltpu.make_async_copy(gout.at[i], grads.at[seq], g_recv).start()

        @pl.when(jnp.logical_not(is_self(i)))
        def _():
            grad_copy(i).start()

        return 0

    lax.fori_loop(0, SHARDS, start_grads, 0)

    def param_copy(i):
        target = (ch + i) % WAYS
        return pltpu.make_async_remote_copy(
            src_ref=pars.at[target],
            dst_ref=params,
            send_sem=p_send.at[i],
            recv_sem=p_recv,
            device_id={"ch": target},
            device_id_type=MESH,
        )

    @pl.when(at_home)
    def _():
        pltpu.make_async_copy(pars.at[ch], params, p_recv).start()
        for i in range(1, WAYS):
            param_copy(i).start()

    weight_in.wait()
    done = [project(0, 0)]

    def follow(dx, dz):
        done.append(project(dx, dz))
        deliver(done[-2])

    for v in range(2):
        arrive(v, "P1+")
        send(v, "P2+")
        send(v, "Q1+1")
        send(v, "Q1-1")
        arrive(v, "P1-")
        send(v, "P2-")
        send(v, "Q1+2")
        send(v, "Q1-2")
    for v in range(2):
        arrive(v, "Q1+0")
        send(v, "Q2+0")
        arrive(v, "Q1-0")
        send(v, "Q2-0")
    for v in range(2):
        arrive(v, "P2+")
        send(v, "Q1+3a")
        send(v, "Q1-3a")
        arrive(v, "P2-")
        send(v, "Q1+3b")
        send(v, "Q1-3b")
    for dx, dz in ((-1, 0), (1, 0), (0, -1), (0, 1)):
        follow(dx, dz)
    for j in (1, 2):
        for v in range(2):
            arrive(v, f"Q1+{j}")
            send(v, f"Q2+{j}")
            arrive(v, f"Q1-{j}")
            send(v, f"Q2-{j}")
    for dx, dz in ((-1, -1), (-1, 1)):
        follow(dx, dz)
    for v in range(2):
        arrive(v, "Q1+3a")
        send(v, "Q2+3")
        arrive(v, "Q1-3b")
        send(v, "Q2-3")
    for dx, dz in ((1, -1), (1, 1)):
        follow(dx, dz)
    for v in range(2):
        arrive(v, "Q1+3b")
        arrive(v, "Q1-3a")
        arrive(v, "Q2+0")
        arrive(v, "Q2-0")
    for dx, dz in ((2, 0), (0, 2)):
        follow(dx, dz)
    for v in range(2):
        for j in (1, 2):
            arrive(v, f"Q2+{j}")
            arrive(v, f"Q2-{j}")
    for dx, dz in ((2, -1), (2, 1), (-1, 2), (1, 2)):
        follow(dx, dz)
    for v in range(2):
        arrive(v, "Q2+3")
        arrive(v, "Q2-3")
    follow(2, 2)
    deliver(done[-1])

    pltpu.make_async_copy(gout, grads, g_recv).wait()
    pltpu.make_async_copy(pars.at[0], params, p_recv).wait()
    for i in range(1, WAYS):
        pltpu.make_async_copy(parts.at[0], parts.at[i], r_recv.at[i]).wait()
    mix(count, params, parts, grads, kvs, gms, grs, proj, convs, corrs, small, full.at[0])

    width = SHARDS * CHUNK
    left, right = pl.ds(0, width // 2), pl.ds(width // 2, width // 2)

    def group_copy(n, source, target_slot, step, other, lanes=None):
        target = ring(y, step) * 2 + (1 - core if other else core)
        src, dst = full.at[source], full.at[target_slot]
        if lanes is not None:
            src, dst = full.at[source, :, lanes], full.at[target_slot, :, lanes]
        return pltpu.make_async_remote_copy(
            src_ref=src, dst_ref=dst, send_sem=a_send.at[n], recv_sem=a_recv.at[n],
            device_id={"ch": target}, device_id_type=MESH,
        )

    moves = [
        group_copy(0, 0, 6, 1, False),
        group_copy(1, 0, 2, -1, False),
        group_copy(2, 0, 1, 0, True),
        group_copy(3, 6, 4, 1, False, left),
        group_copy(4, 2, 4, -1, False, right),
        group_copy(5, 6, 7, 0, True),
        group_copy(6, 2, 3, 0, True),
        group_copy(7, 4, 5, 0, True, left),
        group_copy(8, 4, 5, 0, True, right),
    ]
    for n in (0, 1, 2):
        moves[n].start()

    def small_copy(i):
        return pltpu.make_async_remote_copy(
            src_ref=small,
            dst_ref=shared.at[(seq % 2) * WAYS + ch],
            send_sem=s_send.at[i],
            recv_sem=s_recv,
            device_id={"seq": i, "ch": home},
            device_id_type=MESH,
        )

    def small_self(i):
        return jnp.logical_and(i == seq, at_home)

    def start_small(i, _):
        @pl.when(small_self(i))
        def _():
            pltpu.make_async_copy(small, shared.at[(seq % 2) * WAYS + ch], s_recv).start()

        @pl.when(jnp.logical_not(small_self(i)))
        def _():
            small_copy(i).start()

        return 0

    lax.fori_loop(0, SHARDS, start_small, 0)

    tile = 256

    def weight_rows(slots, first, last):
        def body(n, _):
            lanes = pl.ds(pl.multiple_of(n * tile, tile), tile)
            left_side = jnp.concatenate([full[s] for s in slots], 0)
            right_side = every[:, :, lanes].reshape(width, tile)
            out = mul(left_side, right_side)
            for at, slot in enumerate(slots):
                owner = ring(y, slot // 2) * 2 + (1 - core if slot % 2 else core)
                rows = pl.ds(pl.multiple_of(owner * TRIO, TRIO), TRIO)
                wgrad[rows, lanes] = out[at * TRIO : (at + 1) * TRIO]
            return 0

        lax.fori_loop(first, last, body, 0)

    moves[0].wait_recv()
    moves[3].start()
    moves[5].start()
    moves[1].wait_recv()
    moves[4].start()
    moves[6].start()
    moves[2].wait_recv()
    weight_rows((0, 1, 2, 6), 0, 2)
    moves[3].wait_recv()
    moves[7].start()
    moves[4].wait_recv()
    moves[8].start()
    weight_rows((0, 1, 2, 6), 2, 4)
    for n in (5, 6, 7, 8):
        moves[n].wait_recv()
    weight_rows((3, 7, 4, 5), 0, 4)

    pltpu.make_async_copy(shared, shared, s_recv).wait()
    for move in moves:
        move.wait_send()
    for v in range(2):
        for name, _ in names:
            feature_copy(v, name, False).wait_send()
    for i in range(1, WAYS):
        pltpu.make_async_copy(parts.at[0], parts.at[i], r_send.at[i]).wait()

    def end_small(i, _):
        @pl.when(jnp.logical_not(is_self(i)))
        def _():
            grad_copy(i).wait_send()

        @pl.when(jnp.logical_not(small_self(i)))
        def _():
            small_copy(i).wait_send()

        return 0

    lax.fori_loop(0, SHARDS, end_small, 0)

    @pl.when(at_home)
    def _():
        for i in range(1, WAYS):
            param_copy(i).wait_send()


def local(features, qkv_weight, grad_out, residues, log_rates, skip_gain):
    seq = lax.axis_index("seq")
    width = features.shape[1]
    count = qkv_weight.shape[0] // WAYS
    spare = ROWS - count
    weight = qkv_weight.reshape(WAYS, count, 3, width).transpose(0, 2, 1, 3)
    weight = jnp.pad(weight, ((0, 0), (0, 0), (0, spare), (0, 0))).reshape(WAYS * TRIO, width)
    grads = jnp.pad(grad_out.reshape(2 * WAYS, count, CHUNK), ((0, 0), (0, spare), (0, 0)))

    def picked(rows):
        halves = rows.reshape(2, WAYS, count, *rows.shape[1:])
        return lax.dynamic_index_in_dim(halves, seq % 2, 0, keepdims=False)

    def tiled(block):
        return jnp.pad(block, ((0, 0), (0, ROWS - block.shape[1]), (0, CHUNK - block.shape[2])))

    rates_p, residues_p, gain_p = picked(log_rates), picked(residues), picked(skip_gain)
    pars = jnp.concatenate(
        [
            tiled(rates_p.transpose(0, 2, 1)),
            tiled(residues_p.transpose(0, 2, 1)),
            tiled(jnp.tile(rates_p, (1, 1, 3))),
            tiled(residues_p),
            tiled(jnp.broadcast_to(gain_p[:, :, None], (*gain_p.shape, CHUNK))),
        ],
        axis=1,
    )
    anywhere = pl.BlockSpec(memory_space=pl.ANY)
    vmem = pl.BlockSpec(memory_space=pltpu.VMEM)
    dma = pltpu.SemaphoreType.DMA
    tokens = SHARDS * CHUNK
    chunked = pltpu.VMEM((SHARDS, ROWS, CHUNK), F32)
    wgrad, shared = pl.pallas_call(
        functools.partial(kernel, count),
        out_shape=(
            jax.ShapeDtypeStruct((WAYS * TRIO, width), F32),
            jax.ShapeDtypeStruct((2 * WAYS, ROWS, CHUNK), F32),
        ),
        in_specs=[anywhere, anywhere, vmem, vmem],
        out_specs=(vmem, vmem),
        scratch_shapes=[
            pltpu.VMEM((SHARDS, CHUNK, width), BF16),
            pltpu.VMEM((WAYS * TRIO, width), BF16),
            pltpu.VMEM((SHARDS, WAYS, TRIO, CHUNK), BF16),
            pltpu.VMEM((WAYS, SHARDS, TRIO, CHUNK), BF16),
            pltpu.VMEM((SHARDS, ROWS, CHUNK), BF16),
            pltpu.VMEM((PARAM_ROWS, CHUNK), F32),
            chunked,
            chunked,
            chunked,
            pltpu.VMEM((SHARDS, TRIO, CHUNK), BF16),
            chunked,
            chunked,
            pltpu.VMEM((ROWS, CHUNK), F32),
            pltpu.VMEM((WAYS, TRIO, tokens), BF16),
            dma((2,)),
            dma((2, 22)),
            dma((2, 22)),
            dma((WAYS,)),
            dma((WAYS,)),
            dma((SHARDS,)),
            dma,
            dma((WAYS,)),
            dma,
            dma((9,)),
            dma((9,)),
            dma((SHARDS,)),
            dma,
        ],
        compiler_params=pltpu.CompilerParams(
            collective_id=0, has_side_effects=True, vmem_limit_bytes=48 * 2**20
        ),
    )(features, weight, grads, pars)
    weight_grad = wgrad.reshape(WAYS, 3, ROWS, width)[:, :, :count].transpose(0, 2, 1, 3)
    weight_grad = weight_grad.reshape(qkv_weight.shape)
    small = shared[:, :count].reshape(residues.shape[0], CHUNK)
    order = residues.shape[1]
    moment = small[:, order : 2 * order] + small[:, 2 * order : 3 * order]
    rate_grad = -residues * jnp.exp(log_rates) * moment
    return weight_grad, small[:, :order], rate_grad, small[:, 3 * order]


def solution(mesh):
    placed = (
        P("seq", "ch"),
        P("seq", None, "ch"),
        P("ch", "seq"),
        P("ch", None),
        P("ch", None),
        P("ch"),
    )
    return jax.shard_map(
        local,
        mesh=mesh,
        in_specs=placed,
        out_specs=(P("seq", None, "ch"), P("ch", None), P("ch", None), P("ch")),
        check_vma=False,
    )
```

time: 244 us -> 75.3 us (0.31)
  local copies, waits for them, and re-layouts: 83.2 us -> 7.23 us
  Pallas kernels: 0 us -> 66.8 us
  blocking collectives: 60.4 us -> 0 us
  waiting for transfers between devices: 29.8 us -> 0 us
  other arithmetic: 22.4 us -> 0.12 us
  starting transfers between devices: 19.2 us -> 0 us
  matrix products: 13.6 us -> 0 us
  between operations: 14.5 us -> 0.9 us
    pallas_call x0 -> x1, Pallas kernels: none -> 66.8 us  [local(): pl.pallas_call(functools.partial(kernel, count), out_shape=(jax.ShapeDtyp...]
    gather x2 -> x0, local copies, waits for them, and re-layouts: 61.2 us -> none  [toeplitz(): jnp.take(taps, jnp.maximum(lag, 0).reshape(-1), axis=1)]
    all_gather x2 -> x0, blocking collectives: 60.4 us -> none  [the longest x1 35.8 us: local(): gathered = lax.all_gather(small, ('seq', 'ch'), axis=0, tiled=True)]
    all_to_all x3 -> x0, starting transfers between devices: 19.2 us -> none  [the longest x2 14 us: to_owner(): lax.all_to_all(picked, 'ch', split_axis=0, concat_axis=0, tiled=True)]
    all_to_all x3 -> x0, waiting for transfers between devices: 16.3 us -> none  [the longest x1 16.3 us: local(): lax.all_to_all(tiles, 'ch', split_axis=0, concat_axis=0, tiled=True)]
    dot_general x13 -> x0, matrix products: 13.6 us -> none  [the longest x1 6.24 us: local(): jnp.einsum('cgt,td->cgd', full, every, preferred_element_type=jnp.float32)]
    all_gather x2 -> x0, waiting for transfers between devices: 12.8 us -> none  [the longest x1 12.8 us: local(): every = lax.all_gather(features, 'seq', axis=0, tiled=True)]
    unnamed x17 -> x0, other arithmetic: 11.9 us -> none
  transfers between devices with their start and end apart: 5 -> 0, of which waited for: 2 -> 0; matrix products, arithmetic and copies ran while one was open for 8% -> 0% of each run, Pallas kernels for 0% -> 0%
where the time goes in v2:
time: 75.3 us; the launch traced here: 75 us
  Pallas kernels  66.8 us (89%)
  local copies, waits for them, and re-layouts  7.23 us (10%)
  between operations  0.9 us (1%)
    pallas_call x1, Pallas kernels, local(): pl.pallas_call(functools.partial(kernel, count), out_shape=(jax.ShapeDtyp...  66.8 us
    unnamed x21, local copies, waits for them, and re-layouts  2.32 us
    reshape x3, local copies, waits for them, and re-layouts, picked(): halves = rows.reshape(2, WAYS, count, *rows.shape[1:])  1.78 us

profile of v2, /device:TPU:1, one launch (start us, length us, event | category | flops | bytes accessed | tf_op | source)
XLA Modules:
  0.0 75.0 jit_solution(1769157417447254970)
XLA Ops:
  0.6 0.0 copy-start.5
  0.6 0.0 copy-start.1
  0.7 0.9 %reshape.45 = f32[2,8,13,16]{2,1,0,3:T(8,128)S(1)} reshape(f32[208,16]{0,1:T(8,128)} %param.10) | data formatting | bytes 26624 | tf_op jit(solution)/shard_map/reshape | solution.py:519
  1.6 0.8 %reshape.46 = f32[2,8,13,16]{2,1,0,3:T(8,128)S(1)} reshape(f32[208,16]{0,1:T(8,128)} %param.9) | data formatting | bytes 26624 | tf_op jit(solution)/shard_map/reshape | solution.py:519
  2.5 0.1 copy.22
  2.6 0.1 tile.4
  2.7 0.1 tile.10
  2.9 0.1 copy.21
  3.0 0.0 copy-done.5
  3.0 0.1 reshape.47
  3.1 0.1 broadcast_in_dim.9
  3.2 0.0 copy-done.1
  3.2 0.2 reshape.42
  3.4 0.0 copy-start.4
  3.4 0.0 copy-start
  3.5 0.1 copy.32
  3.5 0.1 pad.27.clone
  3.6 0.6 copy-done.4
  4.3 0.1 copy-done
  4.4 66.8 %shard_map.93 = (f32[384,1024]{1,0:T(8,128)S(1)}, f32[16,16,128]{2,1,0:T(8,128)S(1)}) custom-call(bf16[128,1024]{1,0:T(8,128)(2,1)S(1)} %copy-done, bf16[384,1024]{1,0:T(8,128)(2,1)S(1)} %bitcast.28, bf16[16,16,128]{2,1,0:T(8,128)(2,1)S(1)} %pad.28.gout, f32[8,80,128]{2,1,0:T(8,128)S(1)} %pad_dynamic-update-slice_fusion.1.pars), custom_call_target="tpu_custom_call" | custom-call | tf_op jit(solution)/shard_map/pallas_call | solution.py:541
  71.2 0.1 copy_bitcast_fusion
  71.3 0.0 copy-start.3
  71.3 0.0 copy-start.2
  71.3 1.2 %reshape.49 = f32[104,3,1024]{2,0,1:T(8,128)} reshape(f32[8,13,3,1024]{3,1,0,2:T(8,128)S(1)} %copy_bitcast_fusion) | data formatting | bytes 2555904 | tf_op jit(solution)/shard_map/reshape | solution.py:583
  72.6 0.0 copy-done.3
  72.6 0.1 copy.27
  72.7 0.0 copy-done.2
  72.7 0.1 copy.26
  72.8 0.1 fusion
  72.9 0.7 copy.28
  73.6 0.7 copy.29
  74.3 0.7 slice_reduce_fusion
  (14 shorter events, 0.2 us)
Async XLA Ops:
  0.6 2.4 %copy-start.5 = (f32[208]{0:T(256)S(1)}, f32[208]{0:T(256)}, u32[]{:S(2)}) copy-start(f32[208]{0:T(256)} %param.11) | copy-start | bytes 2500
  0.6 2.6 %copy-start.1 = (bf16[104,3,1024]{2,0,1:T(8,128)(2,1)S(1)}, bf16[104,3,1024]{2,0,1:T(8,128)(2,1)}, u32[]{:S(2)}) copy-start(bf16[104,3,1024]{2,0,1:T(8,128)(2,1)} %param.7) | copy-start | bytes 1916932
  3.4 0.8 %copy-start.4 = (bf16[208,128]{1,0:T(8,128)(2,1)S(1)}, bf16[208,128]{1,0:T(8,128)(2,1)}, u32[]{:S(2)}) copy-start(bf16[208,128]{1,0:T(8,128)(2,1)} %param.8) | copy-start | bytes 159748
  3.4 1.0 %copy-start = (bf16[128,1024]{1,0:T(8,128)(2,1)S(1)}, bf16[128,1024]{1,0:T(8,128)(2,1)}, u32[]{:S(2)}) copy-start(bf16[128,1024]{1,0:T(8,128)(2,1)} %feat.1) | copy-start | bytes 786436
  71.3 1.3 %copy-start.3 = (f32[208,16]{0,1:T(8,128)S(1)}, f32[208,16]{0,1:T(8,128)}, u32[]{:S(2)}) copy-start(f32[208,16]{0,1:T(8,128)} %param.10) | copy-start | bytes 39940
  71.3 1.4 %copy-start.2 = (f32[208,16]{0,1:T(8,128)S(1)}, f32[208,16]{0,1:T(8,128)}, u32[]{:S(2)}) copy-start(f32[208,16]{0,1:T(8,128)} %param.9) | copy-start | bytes 39940

commit v3 on v2

v3 whole, which is shorter than its diff:
```python
import functools

import jax
import jax.numpy as jnp
from jax import lax
from jax.experimental import pallas as pl
from jax.experimental.pallas import tpu as pltpu
from jax.sharding import PartitionSpec as P

F32, BF16 = jnp.float32, jnp.bfloat16
CHUNK = 128
SIDE = 4
SHARDS = SIDE * SIDE
WAYS = 2 * SIDE
ROWS = 16
TRIO = 40
STATE = 16
MESH = pl.DeviceIdType.MESH
PARAM_ROWS = 40

NT = (((1,), (1,)), ((), ()))
TN = (((0,), (0,)), ((), ()))
NN = (((1,), (0,)), ((), ()))


def mul(a, b, dims=NN):
    return lax.dot_general(a, b, dims, preferred_element_type=F32)


def exact(a, b, dims=NN):
    return lax.dot_general(a, b, dims, precision="highest", preferred_element_type=F32)


def iota(shape, dim):
    return lax.broadcasted_iota(jnp.int32, shape, dim)


def chosen(shape, rule, kind=BF16):
    return rule(iota(shape, 0), iota(shape, 1)).astype(kind)


def sum_partials(parts, grads, projf, projr, gradf):
    flip = chosen((CHUNK, CHUNK), lambda r, c: r + c == CHUNK - 1)

    def body(k, _):
        total = parts[0, k].astype(F32)
        for way in range(1, WAYS):
            total = total + parts[way, k].astype(F32)
        rounded = total.astype(BF16)
        projf[k] = rounded.astype(F32)
        projr[k] = mul(rounded, flip)
        gradf[k] = grads[k].astype(F32)
        return 0

    lax.fori_loop(0, SHARDS, body, 0, unroll=4)


def carry(values, step, lagged, reverse):
    row = iota(values.shape, 0)
    shape = values.shape
    decay = jnp.broadcast_to(step, shape)
    reach = 1
    while reach < shape[0]:
        amount = shape[0] - reach if reverse else reach
        keep = row < shape[0] - reach if reverse else row >= reach
        near = jnp.where(keep, decay * pltpu.roll(values, amount, 0), 0.0)
        if lagged is not None:
            moved = jnp.where(keep, decay * pltpu.roll(lagged, amount, 0), 0.0)
            lagged = lagged + moved + (CHUNK * reach) * near
        values = values + near
        decay = decay * decay
        reach *= 2
    return values, lagged


def before(values, reverse):
    row = iota(values.shape, 0)
    last = values.shape[0] - 1
    if reverse:
        return jnp.where(row < last, pltpu.roll(values, last, 0), 0.0)
    return jnp.where(row >= 1, pltpu.roll(values, 1, 0), 0.0)


def select_params(count, offset, params, cols, rows, gains):
    lanes = params.shape[1]
    down = chosen((lanes, CHUNK), lambda r, c: (r == c + offset) & (c < count), F32)
    across = chosen((ROWS, lanes), lambda r, c: (c == r + offset) & (r < count), F32)
    cols[...] = exact(params[0 : 2 * STATE], down)
    rates = params[0:STATE]
    rows[:, 0 : 3 * STATE] = exact(across, jnp.concatenate([rates, rates, rates], 0), NT)
    gain = jnp.broadcast_to(params[2 * STATE : 2 * STATE + 1], (CHUNK, lanes))
    gains[...] = exact(across, gain, NT)


def tables_of(c, cols, bands, tables):
    lane = iota((STATE, CHUNK), 1).astype(F32)
    rates = jnp.exp(cols[0:STATE, c : c + 1])
    residues = cols[STATE : 2 * STATE, c : c + 1]
    near = jnp.exp(-rates * lane)
    far = jnp.exp(-rates * (CHUNK - lane))
    weighted = residues * near
    taps = jnp.sum(weighted, axis=0, keepdims=True)
    upper = iota((CHUNK, CHUNK), 1) >= iota((CHUNK, CHUNK), 0)
    spread = pltpu.roll(jnp.broadcast_to(taps, (CHUNK, CHUNK)), 0, 1, stride=1, stride_axis=0)
    bands[c] = jnp.where(upper, spread, 0.0).astype(BF16)
    far_lag = (far * (CHUNK - lane)).astype(BF16)
    blocks = [near, near * lane, near, far, far, far, None, None, None, weighted, residues * far]
    for at, block in enumerate(blocks):
        tables[c, at * STATE : (at + 1) * STATE] = far_lag if block is None else block.astype(BF16)


def mix_channels(group, rows, gains, bands, tables, projf, projr, gradf, small, skips, outs):
    lower = iota((CHUNK, CHUNK), 1) <= iota((CHUNK, CHUNK), 0)
    third = iota((SHARDS, 3 * STATE), 1) < 2 * STATE
    kvs, gms, firsts = {}, {}, {}
    for c in group:
        kv = projf[:, 3 * c + 1, :] * projf[:, 3 * c + 2, :]
        gm = gradf[:, c, :] * projf[:, 3 * c, :]
        back = projr[:, 3 * c + 1, :] * projr[:, 3 * c + 2, :]
        kvs[c], gms[c] = kv, gm
        skips[c : c + 1] = jnp.sum(kv * gm, axis=0, keepdims=True)
        kv, gm, back = kv.astype(BF16), gm.astype(BF16), back.astype(BF16)
        firsts[c] = (
            mul(kv, tables[c, 3 * STATE : 6 * STATE], NT),
            mul(kv, tables[c, 6 * STATE : 9 * STATE], NT),
            mul(gm, tables[c, 0 : 3 * STATE], NT),
            mul(back, gm, TN),
            mul(kv, bands[c]),
            mul(gm, bands[c], NT),
        )
    seconds = {}
    for c in group:
        tails, tails_lag, heads, product, _, _ = firsts[c]
        step = jnp.exp(-CHUNK * jnp.exp(rows[c : c + 1, 0 : 3 * STATE]))
        states, states_lag = carry(tails, step, tails_lag, False)
        states, states_lag = before(states, False), before(states_lag, False)
        inter = jnp.sum(heads * jnp.where(third, states, states_lag), axis=0, keepdims=True)
        adjoints, _ = carry(heads[:, 0:STATE], step[:, 0:STATE], None, True)
        adjoints = before(adjoints, True)
        skewed = pltpu.roll(product, 1, 1, stride=1, stride_axis=0)
        sums = jnp.sum(jnp.where(lower, skewed, 0.0), axis=0, keepdims=True)
        wide = jnp.broadcast_to(sums, (ROWS, CHUNK)).astype(BF16)
        seconds[c] = (
            mul(states[:, 0:STATE].astype(BF16), tables[c, 9 * STATE : 10 * STATE]),
            mul(adjoints.astype(BF16), tables[c, 10 * STATE : 11 * STATE]),
            mul(wide, tables[c, 0 : 2 * STATE], NT),
            inter,
        )
    for c in group:
        conv, corr, intra, inter = seconds[c]
        gain = gains[c : c + 1]
        conv = conv + firsts[c][4] + gain * kvs[c]
        grad_mix = corr + firsts[c][5] + gain * gms[c]
        outs[:, 3 * c, :] = gradf[:, c, :] * conv
        outs[:, 3 * c + 1, :] = grad_mix * projf[:, 3 * c + 2, :]
        outs[:, 3 * c + 2, :] = grad_mix * projf[:, 3 * c + 1, :]
        small[c : c + 1, 0 : 3 * STATE] = inter
        small[c : c + 1, 0 : 2 * STATE] += intra[0:1]


def pack(outs, mine, first, last):
    for k in range(SHARDS):
        mine[first:last, k * CHUNK : (k + 1) * CHUNK] = outs[k, first:last].astype(BF16)


def finish_small(count, small, skips):
    lane = iota((ROWS, CHUNK), 1)
    row = iota((ROWS, CHUNK), 0)
    summed = jnp.sum(skips[...], axis=1, keepdims=True)
    filled = jnp.where(lane == 3 * STATE, summed, small[...])
    small[...] = jnp.where(row < count, filled, 0.0)


def kernel(
    count, feat, weight, gout, rates_t, residues_t, gain, wgrad, residue_out, rate_out, skip_out,
    every, wraw, wbuf, graw, gbuf, packed, partial, parts, grads, params, cols, rows, gains, bands,
    tables, projf, projr, gradf, outs, small, skips, shared, full, ordered_grads,
    local_sem, f_send, f_recv, r_send, r_recv, g_send, g_recv, p_send, p_recv, a_send, a_recv,
    s_send, s_recv,
):
    seq, ch = lax.axis_index("seq"), lax.axis_index("ch")
    x, z = seq // SIDE, seq % SIDE
    y, core = ch // 2, ch % 2
    home = seq // 2
    at_home = ch == home

    feat_in = pltpu.make_async_copy(feat, every.at[seq], local_sem.at[0])
    weight_in = pltpu.make_async_copy(weight, wraw, local_sem.at[1])
    grads_in = pltpu.make_async_copy(gout, graw, local_sem.at[2])
    small_in = [
        pltpu.make_async_copy(rates_t, packed.at[pl.ds(0, STATE)], local_sem.at[3]),
        pltpu.make_async_copy(residues_t, packed.at[pl.ds(STATE, STATE)], local_sem.at[4]),
        pltpu.make_async_copy(gain, packed.at[pl.ds(2 * STATE, 8)], local_sem.at[5]),
    ]
    feat_in.start()
    for copy in small_in:
        copy.start()
    weight_in.start()
    grads_in.start()

    def ring(value, step):
        return (value + step + SIDE) % SIDE

    def place(v, p, q):
        return p * SIDE + q if v == 0 else q * SIDE + p

    def spot(v):
        return (x, z) if v == 0 else (z, x)

    barrier = pltpu.get_barrier_semaphore()

    def greet(s, c):
        pl.semaphore_signal(barrier, inc=1, device_id={"seq": s, "ch": c}, device_id_type=MESH)

    for v in range(2):
        p, q = spot(v)
        for step in (-1, 1):
            greet(place(v, ring(p, step), q), ch)
    for i in range(1, WAYS):
        greet(seq, (ch + i) % WAYS)
    small[...] = jnp.zeros_like(small)
    skips[...] = jnp.zeros_like(skips)
    outs[:, TRIO - 1, :] = jnp.zeros((SHARDS, CHUNK), F32)
    pl.semaphore_wait(barrier, 4 + WAYS - 1)

    half, quarter = CHUNK // 2, CHUNK // 4
    offs = (0, -1, 1, 2)

    def piece(v, part):
        start = v * half + (quarter if part == "b" else 0)
        return pl.ds(start, half if part == "h" else quarter)

    names = [("P1+", "h"), ("P1-", "h"), ("P2+", "a"), ("P2-", "b")]
    for j in range(3):
        names += [(f"Q1+{j}", "h"), (f"Q1-{j}", "h"), (f"Q2+{j}", "a"), (f"Q2-{j}", "b")]
    names += [("Q1+3a", "a"), ("Q1+3b", "b"), ("Q1-3a", "a"), ("Q1-3b", "b")]
    names += [("Q2+3", "a"), ("Q2-3", "b")]
    number = {name: n for n, (name, _) in enumerate(names)}
    piece_of = dict(names)

    def feature_copy(v, name, arriving):
        p, q = spot(v)
        step = 1 if name[2] == "+" else -1
        hops = int(name[1]) - 1 + (1 if arriving else 0)
        if name[0] == "P":
            source = place(v, ring(p, -step * hops), q)
            target = place(v, ring(p, step), q)
        else:
            source = place(v, ring(p, offs[int(name[3])]), ring(q, -step * hops))
            target = place(v, p, ring(q, step))
        rows = piece(v, piece_of[name])
        return pltpu.make_async_remote_copy(
            src_ref=every.at[source, rows],
            dst_ref=every.at[source, rows],
            send_sem=f_send.at[v, number[name]],
            recv_sem=f_recv.at[v, number[name]],
            device_id={"seq": target},
            device_id_type=MESH,
        )

    def send(v, name):
        feature_copy(v, name, False).start()

    def arrive(v, name):
        feature_copy(v, name, True).wait_recv()

    def owner_copy(shard, i):
        target = (ch + i) % WAYS
        return pltpu.make_async_remote_copy(
            src_ref=partial.at[shard, target],
            dst_ref=parts.at[i, shard],
            send_sem=r_send.at[i],
            recv_sem=r_recv.at[i],
            device_id={"ch": target},
            device_id_type=MESH,
        )

    def shard_at(dx, dz):
        return ring(x, dx) * SIDE + ring(z, dz)

    def project(dx, dz):
        shard = shard_at(dx, dz)
        out = mul(wbuf[...], every[shard], NT).astype(BF16).reshape(WAYS, TRIO, CHUNK)
        partial[shard] = out
        parts[0, shard] = partial[shard, ch]
        return shard

    def deliver(shard):
        for i in range(1, WAYS):
            owner_copy(shard, i).start()

    feat_in.wait()
    for v in range(2):
        send(v, "P1+")
        send(v, "P1-")
    for v in range(2):
        send(v, "Q1+0")
        send(v, "Q1-0")

    def param_copy(i):
        return pltpu.make_async_remote_copy(
            src_ref=packed,
            dst_ref=params,
            send_sem=p_send.at[i],
            recv_sem=p_recv,
            device_id={"ch": (ch + i) % WAYS},
            device_id_type=MESH,
        )

    for copy in small_in:
        copy.wait()

    @pl.when(at_home)
    def _():
        pltpu.make_async_copy(packed, params, p_recv).start()
        for i in range(1, WAYS):
            param_copy(i).start()

    def grad_copy(shard, c):
        slot = (shard % 2) * WAYS + c
        return pltpu.make_async_remote_copy(
            src_ref=gbuf.at[slot],
            dst_ref=grads.at[seq],
            send_sem=g_send.at[slot],
            recv_sem=g_recv,
            device_id={"seq": shard, "ch": c},
            device_id_type=MESH,
        )

    def give_grads(dx, dz):
        shard = shard_at(dx, dz)

        @pl.when(shard // 2 == ch)
        def _():
            def one(c, _):
                if dx or dz:
                    grad_copy(shard, c).start()
                else:
                    @pl.when(c == ch)
                    def _():
                        slot = (shard % 2) * WAYS + c
                        pltpu.make_async_copy(gbuf.at[slot], grads.at[seq], g_recv).start()

                    @pl.when(c != ch)
                    def _():
                        grad_copy(shard, c).start()

                return 0

            lax.fori_loop(0, WAYS, one, 0)

    weight_in.wait()
    block = count * WAYS
    ordered = None
    for g in range(3):
        pick = chosen(
            (WAYS * TRIO, block),
            lambda r, c: (r % TRIO == 3 * (c % count) + g) & (r // TRIO == c // count),
        )
        part = mul(pick, wraw[g])
        ordered = part if ordered is None else ordered + part
    wbuf[...] = ordered.astype(BF16)
    grads_in.wait()
    pick = chosen(
        (2 * WAYS * ROWS, 2 * block), lambda r, c: (r // ROWS == c // count) & (r % ROWS == c % count)
    )
    gbuf[...] = mul(pick, graw[...]).astype(BF16).reshape(2 * WAYS, ROWS, CHUNK)

    done = [project(0, 0)]
    give_grads(0, 0)

    def follow(dx, dz):
        done.append(project(dx, dz))
        deliver(done[-2])

    prepared = []

    def prepare(number_of):
        for _ in range(number_of):
            if len(prepared) < count:
                tables_of(len(prepared), cols, bands, tables)
                prepared.append(0)

    for v in range(2):
        near = ((-1, 0), (1, 0)) if v == 0 else ((0, -1), (0, 1))
        arrive(v, "P1+")
        send(v, "P2+")
        send(v, "Q1+1")
        send(v, "Q1-1")
        give_grads(*near[0])
        arrive(v, "P1-")
        send(v, "P2-")
        send(v, "Q1+2")
        send(v, "Q1-2")
        give_grads(*near[1])
    pltpu.make_async_copy(packed, params, p_recv).wait()
    for v in range(2):
        arrive(v, "Q1+0")
        send(v, "Q2+0")
        arrive(v, "Q1-0")
        send(v, "Q2-0")
    offset = (seq % 2) * block + ch * count
    select_params(count, offset, params, cols, rows, gains)
    for v in range(2):
        arrive(v, "P2+")
        send(v, "Q1+3a")
        send(v, "Q1-3a")
        arrive(v, "P2-")
        send(v, "Q1+3b")
        send(v, "Q1-3b")
        give_grads(*((2, 0) if v == 0 else (0, 2)))
    for dx, dz in ((-1, 0), (1, 0), (0, -1), (0, 1)):
        follow(dx, dz)
    prepare(2)
    for j in (1, 2):
        for v in range(2):
            arrive(v, f"Q1+{j}")
            send(v, f"Q2+{j}")
            arrive(v, f"Q1-{j}")
            send(v, f"Q2-{j}")
        give_grads(-1 if j == 1 else 1, -1)
        give_grads(-1 if j == 1 else 1, 1)
        prepare(2)
    for dx, dz in ((-1, -1), (-1, 1), (1, -1), (1, 1)):
        follow(dx, dz)
        prepare(1)
    for v in range(2):
        arrive(v, "Q1+3a")
        send(v, "Q2+3")
        arrive(v, "Q1-3b")
        send(v, "Q2-3")
        for side in (-1, 1):
            give_grads(*((2, side) if v == 0 else (side, 2)))
    for v in range(2):
        arrive(v, "Q1+3b")
        arrive(v, "Q1-3a")
        arrive(v, "Q2+0")
        arrive(v, "Q2-0")
    for dx, dz in ((2, 0), (0, 2)):
        follow(dx, dz)
        prepare(1)
    for v in range(2):
        for j in (1, 2):
            arrive(v, f"Q2+{j}")
            arrive(v, f"Q2-{j}")
    for dx, dz in ((2, -1), (2, 1), (-1, 2), (1, 2)):
        follow(dx, dz)
    for v in range(2):
        arrive(v, "Q2+3")
        arrive(v, "Q2-3")
    give_grads(2, 2)
    follow(2, 2)
    deliver(done[-1])
    prepare(count)

    pltpu.make_async_copy(gbuf, grads, g_recv).wait()
    for i in range(1, WAYS):
        pltpu.make_async_copy(parts.at[0], parts.at[i], r_recv.at[i]).wait()
    sum_partials(parts, grads, projf, projr, gradf)

    width = SHARDS * CHUNK
    left, right = pl.ds(0, width // 2), pl.ds(width // 2, width // 2)
    whole = pl.ds(0, width)
    tiles = [pl.ds(0, 16), pl.ds(16, 16), pl.ds(32, TRIO - 32)]

    def owner(step, other):
        return ring(y, step) * 2 + (1 - core if other else core)

    def group_copy(t, n, slot, target, lanes):
        return pltpu.make_async_remote_copy(
            src_ref=full.at[slot, tiles[t], lanes],
            dst_ref=full.at[slot, tiles[t], lanes],
            send_sem=a_send.at[t, n],
            recv_sem=a_recv.at[t, n],
            device_id={"ch": target},
            device_id_type=MESH,
        )

    kinds = [
        (0, 1, False, whole),
        (0, -1, False, whole),
        (0, 0, True, whole),
        (1, 1, False, left),
        (-1, -1, False, right),
        (1, 0, True, whole),
        (-1, 0, True, whole),
        (2, 0, True, left),
        (2, 0, True, right),
    ]

    def going(t, n):
        back, step, other, lanes = kinds[n]
        return group_copy(t, n, owner(-back, False), owner(step, other), lanes)

    def coming(t, n):
        back, step, other, lanes = kinds[n]
        return group_copy(t, n, owner(-back - step, other), owner(step, other), lanes)

    def begin(t):
        for n in (0, 1, 2):
            going(t, n).start()

    def relay(t):
        coming(t, 0).wait_recv()
        going(t, 3).start()
        going(t, 5).start()
        coming(t, 1).wait_recv()
        going(t, 4).start()
        going(t, 6).start()

    def relay_far(t):
        coming(t, 3).wait_recv()
        going(t, 7).start()
        coming(t, 4).wait_recv()
        going(t, 8).start()

    mine = full.at[ch]
    groups = [range(0, 6), range(6, 11), range(11, count)]
    edges = [(0, 16), (16, 32), (32, TRIO)]
    for t in range(3):
        mix_channels(
            groups[t], rows, gains, bands, tables, projf, projr, gradf, small, skips, outs
        )
        pack(outs, mine, *edges[t])
        begin(t)
        if t > 0:
            relay(t - 1)
    finish_small(count, small, skips)

    def small_copy(i):
        return pltpu.make_async_remote_copy(
            src_ref=small,
            dst_ref=shared.at[(seq % 2) * WAYS + ch],
            send_sem=s_send.at[i],
            recv_sem=s_recv,
            device_id={"seq": i, "ch": home},
            device_id_type=MESH,
        )

    def small_self(i):
        return jnp.logical_and(i == seq, at_home)

    def start_small(i, _):
        @pl.when(small_self(i))
        def _():
            pltpu.make_async_copy(small, shared.at[(seq % 2) * WAYS + ch], s_recv).start()

        @pl.when(jnp.logical_not(small_self(i)))
        def _():
            small_copy(i).start()

        return 0

    relay_far(0)
    lax.fori_loop(0, SHARDS, start_small, 0)
    relay_far(1)
    relay(2)
    relay_far(2)

    pltpu.make_async_copy(shared, shared, s_recv).wait()
    pick = chosen(
        (2 * WAYS * ROWS, 2 * block),
        lambda r, c: (r // ROWS == c // count) & (r % ROWS == c % count),
        F32,
    )
    turned = exact(shared[...].reshape(2 * WAYS * ROWS, CHUNK), pick, TN)
    moment = turned[STATE : 2 * STATE] + turned[2 * STATE : 3 * STATE]
    residue_out[...] = turned[0:STATE]
    rate_out[...] = -packed[STATE : 2 * STATE] * jnp.exp(packed[0:STATE]) * moment
    skip_out[...] = turned[3 * STATE : 3 * STATE + 1]

    for t in range(3):
        for n in (2, 5, 6, 7, 8):
            coming(t, n).wait_recv()

    tile = 256
    gathered = full[...].reshape(WAYS * TRIO, width)
    sides = []
    for g in range(3):
        pick = chosen(
            (block, WAYS * TRIO),
            lambda r, c: (c % TRIO == 3 * (r % count) + g) & (c // TRIO == r // count),
        )
        sides.append(mul(pick, gathered).astype(BF16))
    for g in range(3):
        ordered_grads[g] = sides[g]

    def weight_columns(n, _):
        lanes = pl.ds(pl.multiple_of(n * tile, tile), tile)
        right_side = every[:, :, lanes].reshape(width, tile)
        for g in range(3):
            wgrad[g, :, lanes] = mul(ordered_grads[g], right_side)
        return 0

    lax.fori_loop(0, every.shape[2] // tile, weight_columns, 0)

    for t in range(3):
        for n in range(9):
            going(t, n).wait_send()
    for v in range(2):
        for name, _ in names:
            feature_copy(v, name, False).wait_send()
    for i in range(1, WAYS):
        pltpu.make_async_copy(parts.at[0], parts.at[i], r_send.at[i]).wait()

    def end_small(i, _):
        shard = 2 * ch + i // WAYS

        @pl.when(jnp.logical_not(jnp.logical_and(shard == seq, i % WAYS == ch)))
        def _():
            grad_copy(shard, i % WAYS).wait_send()

        @pl.when(jnp.logical_not(small_self(i)))
        def _():
            small_copy(i).wait_send()

        return 0

    lax.fori_loop(0, SHARDS, end_small, 0)

    @pl.when(at_home)
    def _():
        for i in range(1, WAYS):
            param_copy(i).wait_send()


def local(features, qkv_weight, grad_out, residues, log_rates, skip_gain):
    width = features.shape[1]
    block = qkv_weight.shape[0]
    count = block // WAYS
    held, order = residues.shape
    weight = qkv_weight.transpose(1, 0, 2)
    gain = jnp.broadcast_to(skip_gain[None], (8, held))
    anywhere = pl.BlockSpec(memory_space=pl.ANY)
    vmem = pl.BlockSpec(memory_space=pltpu.VMEM)
    dma = pltpu.SemaphoreType.DMA
    tokens = SHARDS * CHUNK
    weight_grad, residue_grad, rate_grad, skip_grad = pl.pallas_call(
        functools.partial(kernel, count),
        out_shape=(
            jax.ShapeDtypeStruct((3, block, width), F32),
            jax.ShapeDtypeStruct((order, held), F32),
            jax.ShapeDtypeStruct((order, held), F32),
            jax.ShapeDtypeStruct((1, held), F32),
        ),
        in_specs=[anywhere] * 6,
        out_specs=(vmem,) * 4,
        scratch_shapes=[
            pltpu.VMEM((SHARDS, CHUNK, width), BF16),
            pltpu.VMEM((3, block, width), BF16),
            pltpu.VMEM((WAYS * TRIO, width), BF16),
            pltpu.VMEM((held, CHUNK), BF16),
            pltpu.VMEM((2 * WAYS, ROWS, CHUNK), BF16),
            pltpu.VMEM((PARAM_ROWS, held), F32),
            pltpu.VMEM((SHARDS, WAYS, TRIO, CHUNK), BF16),
            pltpu.VMEM((WAYS, SHARDS, TRIO, CHUNK), BF16),
            pltpu.VMEM((SHARDS, ROWS, CHUNK), BF16),
            pltpu.VMEM((PARAM_ROWS, held), F32),
            pltpu.VMEM((2 * STATE, CHUNK), F32),
            pltpu.VMEM((ROWS, CHUNK), F32),
            pltpu.VMEM((ROWS, CHUNK), F32),
            pltpu.VMEM((ROWS, CHUNK, CHUNK), BF16),
            pltpu.VMEM((ROWS, 11 * STATE, CHUNK), BF16),
            pltpu.VMEM((SHARDS, TRIO, CHUNK), F32),
            pltpu.VMEM((SHARDS, TRIO, CHUNK), F32),
            pltpu.VMEM((SHARDS, ROWS, CHUNK), F32),
            pltpu.VMEM((SHARDS, TRIO, CHUNK), F32),
            pltpu.VMEM((ROWS, CHUNK), F32),
            pltpu.VMEM((ROWS, CHUNK), F32),
            pltpu.VMEM((2 * WAYS, ROWS, CHUNK), F32),
            pltpu.VMEM((WAYS, TRIO, tokens), BF16),
            pltpu.VMEM((3, block, tokens), BF16),
            dma((6,)),
            dma((2, 22)),
            dma((2, 22)),
            dma((WAYS,)),
            dma((WAYS,)),
            dma((SHARDS,)),
            dma,
            dma((WAYS,)),
            dma,
            dma((3, 9)),
            dma((3, 9)),
            dma((SHARDS,)),
            dma,
        ],
        compiler_params=pltpu.CompilerParams(
            collective_id=0, has_side_effects=True, vmem_limit_bytes=48 * 2**20
        ),
    )(features, weight, grad_out, log_rates.T, residues.T, gain)
    return weight_grad.transpose(1, 0, 2), residue_grad.T, rate_grad.T, skip_grad.reshape(held)


def solution(mesh):
    placed = (
        P("seq", "ch"),
        P("seq", None, "ch"),
        P("ch", "seq"),
        P("ch", None),
        P("ch", None),
        P("ch"),
    )
    return jax.shard_map(
        local,
        mesh=mesh,
        in_specs=placed,
        out_specs=(P("seq", None, "ch"), P("ch", None), P("ch", None), P("ch")),
        check_vma=False,
    )
```

time: 75.3 us -> 70 us (0.930); the launches traced: 75 us -> 68.9 us
  Pallas kernels: 66.8 us -> 60.5 us
    pallas_call x1, Pallas kernels: 66.8 us -> 60.5 us  [local(): pl.pallas_call(functools.partial(kernel, count), out_shape=(jax.ShapeDtyp...]
    unnamed x21 -> x14, local copies, waits for them, and re-layouts: 2.32 us -> 7.09 us
    reshape x7 -> x0, local copies, waits for them, and re-layouts: 3.26 us -> none  [the longest x3 1.78 us: picked(): halves = rows.reshape(2, WAYS, count, *rows.shape[1:])]
where the time goes in v3:
time: 70 us; the launch traced here: 68.9 us
  Pallas kernels  60.5 us (86%)
  local copies, waits for them, and re-layouts  7.77 us (11%)
    pallas_call x1, Pallas kernels, local(): pl.pallas_call(functools.partial(kernel, count), out_shape=(jax.ShapeDtyp...  60.5 us
    unnamed x14, local copies, waits for them, and re-layouts  7.09 us

profile of v3, /device:TPU:1, one launch (start us, length us, event | category | flops | bytes accessed | tf_op | source)
XLA Modules:
  0.0 68.9 jit_solution(13808745479404180751)
XLA Ops:
  0.6 0.7 broadcast_in_dim.2.gain
  1.3 0.0 copy-start
  1.3 1.1 %copy-done = bf16[104,3,1024]{2,0,1:T(8,128)(2,1)S(1)} copy-done((bf16[104,3,1024]{2,0,1:T(8,128)(2,1)S(1)}, bf16[104,3,1024]{2,0,1:T(8,128)(2,1)}, u32[]{:S(2)}) %copy-start) | copy-done | bytes 639000
  2.4 0.0 copy-start.1
  2.4 0.9 %copy-done.1 = bf16[128,1024]{1,0:T(8,128)(2,1)S(1)} copy-done((bf16[128,1024]{1,0:T(8,128)(2,1)S(1)}, bf16[128,1024]{1,0:T(8,128)(2,1)}, u32[]{:S(2)}) %copy-start.1) | copy-done | bytes 262168
  3.3 0.0 copy-start.2
  3.3 0.8 %copy-done.2 = bf16[208,128]{1,0:T(8,128)(2,1)S(1)} copy-done((bf16[208,128]{1,0:T(8,128)(2,1)S(1)}, bf16[208,128]{1,0:T(8,128)(2,1)}, u32[]{:S(2)}) %copy-start.2) | copy-done | bytes 53272
  4.2 0.0 copy-start.3
  4.2 0.7 %copy-done.3 = f32[208,16]{0,1:T(8,128)S(1)} copy-done((f32[208,16]{0,1:T(8,128)S(1)}, f32[208,16]{0,1:T(8,128)}, u32[]{:S(2)}) %copy-start.3) | copy-done | bytes 13336
  4.9 0.0 copy-start.4
  4.9 0.7 %copy-done.4 = f32[208,16]{0,1:T(8,128)S(1)} copy-done((f32[208,16]{0,1:T(8,128)S(1)}, f32[208,16]{0,1:T(8,128)}, u32[]{:S(2)}) %copy-start.4) | copy-done | bytes 13336
  5.6 60.5 %shard_map.93 = (f32[3,104,1024]{2,1,0:T(8,128)S(1)}, f32[16,208]{1,0:T(8,128)S(1)}, f32[16,208]{1,0:T(8,128)S(1)}, f32[1,208]{1,0:T(1,128)S(1)}) custom-call(bf16[128,1024]{1,0:T(8,128)(2,1)S(1)} %copy-done.1, bf16[3,104,1024]{2,1,0:T(8,128)(2,1)S(1)} %bitcast.8, bf16[208,128]{1,0:T(8,128)(2,1)S(1)} %copy-done.2, f32[16,208]{1,0:T(8,128)S(1)} %bitcast.9, ...), custom_call_target="tpu_custom_call" | custom-call | tf_op jit(solution)/shard_map/pallas_call | solution.py:638
  66.1 1.0 %copy.14 = f32[104,3,1024]{2,0,1:T(8,128)} copy(f32[104,3,1024]{2,0,1:T(8,128)S(1)} %bitcast.7) | data formatting | bytes 2555904
  67.1 0.6 copy.15
  67.7 0.6 copy.16
  68.4 0.6 copy.17
Async XLA Ops:
  1.3 1.1 %copy-start = (bf16[104,3,1024]{2,0,1:T(8,128)(2,1)S(1)}, bf16[104,3,1024]{2,0,1:T(8,128)(2,1)}, u32[]{:S(2)}) copy-start(bf16[104,3,1024]{2,0,1:T(8,128)(2,1)} %param.7) | copy-start | bytes 1916932
  2.4 0.9 %copy-start.1 = (bf16[128,1024]{1,0:T(8,128)(2,1)S(1)}, bf16[128,1024]{1,0:T(8,128)(2,1)}, u32[]{:S(2)}) copy-start(bf16[128,1024]{1,0:T(8,128)(2,1)} %feat.1) | copy-start | bytes 786436
  3.3 0.8 %copy-start.2 = (bf16[208,128]{1,0:T(8,128)(2,1)S(1)}, bf16[208,128]{1,0:T(8,128)(2,1)}, u32[]{:S(2)}) copy-start(bf16[208,128]{1,0:T(8,128)(2,1)} %gout.1) | copy-start | bytes 159748
  4.2 0.7 %copy-start.3 = (f32[208,16]{0,1:T(8,128)S(1)}, f32[208,16]{0,1:T(8,128)}, u32[]{:S(2)}) copy-start(f32[208,16]{0,1:T(8,128)} %param.10) | copy-start | bytes 39940
  4.9 0.7 %copy-start.4 = (f32[208,16]{0,1:T(8,128)S(1)}, f32[208,16]{0,1:T(8,128)}, u32[]{:S(2)}) copy-start(f32[208,16]{0,1:T(8,128)} %param.9) | copy-start | bytes 39940

commit v4 on v3

--- a/solution.py
+++ b/solution.py
@@ -16,7 +16,7 @@
 TRIO = 40
 STATE = 16
 MESH = pl.DeviceIdType.MESH
-PARAM_ROWS = 40
+PARAM_ROWS = 2 * STATE
 
 NT = (((1,), (1,)), ((), ()))
 TN = (((0,), (0,)), ((), ()))
@@ -81,15 +81,14 @@
     return jnp.where(row >= 1, pltpu.roll(values, 1, 0), 0.0)
 
 
-def select_params(count, offset, params, cols, rows, gains):
+def select_params(count, offset, params, gain, cols, rows, gains):
     lanes = params.shape[1]
     down = chosen((lanes, CHUNK), lambda r, c: (r == c + offset) & (c < count), F32)
     across = chosen((ROWS, lanes), lambda r, c: (c == r + offset) & (r < count), F32)
     cols[...] = exact(params[0 : 2 * STATE], down)
     rates = params[0:STATE]
     rows[:, 0 : 3 * STATE] = exact(across, jnp.concatenate([rates, rates, rates], 0), NT)
-    gain = jnp.broadcast_to(params[2 * STATE : 2 * STATE + 1], (CHUNK, lanes))
-    gains[...] = exact(across, gain, NT)
+    gains[...] = exact(across, jnp.broadcast_to(gain[...], (CHUNK, lanes)), NT)
 
 
 def tables_of(c, cols, bands, tables):
@@ -172,11 +171,11 @@
 
 
 def kernel(
-    count, feat, weight, gout, rates_t, residues_t, gain, wgrad, residue_out, rate_out, skip_out,
-    every, wraw, wbuf, graw, gbuf, packed, partial, parts, grads, params, cols, rows, gains, bands,
-    tables, projf, projr, gradf, outs, small, skips, shared, full, ordered_grads,
+    count, feat, weight, gout, rates_t, residues_t, gain, every, full, shared, packed,
+    wraw, wbuf, graw, gbuf, partial, parts, grads, params, cols, rows, gains, bands,
+    tables, projf, projr, gradf, outs, small, skips, gain_in, gain_got, mine,
     local_sem, f_send, f_recv, r_send, r_recv, g_send, g_recv, p_send, p_recv, a_send, a_recv,
-    s_send, s_recv,
+    s_send, s_recv, hello, k_send, k_recv, store_sem,
 ):
     seq, ch = lax.axis_index("seq"), lax.axis_index("ch")
     x, z = seq // SIDE, seq % SIDE
@@ -190,7 +189,7 @@
     small_in = [
         pltpu.make_async_copy(rates_t, packed.at[pl.ds(0, STATE)], local_sem.at[3]),
         pltpu.make_async_copy(residues_t, packed.at[pl.ds(STATE, STATE)], local_sem.at[4]),
-        pltpu.make_async_copy(gain, packed.at[pl.ds(2 * STATE, 8)], local_sem.at[5]),
+        pltpu.make_async_copy(gain, gain_in, local_sem.at[5]),
     ]
     feat_in.start()
     for copy in small_in:
@@ -264,6 +263,20 @@
     def arrive(v, name):
         feature_copy(v, name, True).wait_recv()
 
+    def hello_round(n):
+        for v in range(2):
+            p, q = spot(v)
+            for step in (-1, 1):
+                pl.semaphore_signal(
+                    hello.at[n],
+                    inc=1,
+                    device_id={"seq": place(v, ring(p, step), q)},
+                    device_id_type=MESH,
+                )
+
+    def hello_wait(n):
+        pl.semaphore_wait(hello.at[n], 4)
+
     def owner_copy(shard, i):
         target = (ch + i) % WAYS
         return pltpu.make_async_remote_copy(
@@ -296,6 +309,7 @@
     for v in range(2):
         send(v, "Q1+0")
         send(v, "Q1-0")
+    hello_round(0)
 
     def param_copy(i):
         return pltpu.make_async_remote_copy(
@@ -307,14 +321,26 @@
             device_id_type=MESH,
         )
 
+    def gain_copy(i):
+        return pltpu.make_async_remote_copy(
+            src_ref=gain_in,
+            dst_ref=gain_got,
+            send_sem=k_send.at[i],
+            recv_sem=k_recv,
+            device_id={"ch": (ch + i) % WAYS},
+            device_id_type=MESH,
+        )
+
     for copy in small_in:
         copy.wait()
 
     @pl.when(at_home)
     def _():
         pltpu.make_async_copy(packed, params, p_recv).start()
+        pltpu.make_async_copy(gain_in, gain_got, k_recv).start()
         for i in range(1, WAYS):
             param_copy(i).start()
+            gain_copy(i).start()
 
     def grad_copy(shard, c):
         slot = (shard % 2) * WAYS + c
@@ -327,27 +353,19 @@
             device_id_type=MESH,
         )
 
-    def give_grads(dx, dz):
-        shard = shard_at(dx, dz)
-
-        @pl.when(shard // 2 == ch)
+    def is_self(i):
+        return jnp.logical_and(2 * ch + i // WAYS == seq, i % WAYS == ch)
+
+    def give_grads(i, _):
+        @pl.when(is_self(i))
         def _():
-            def one(c, _):
-                if dx or dz:
-                    grad_copy(shard, c).start()
-                else:
-                    @pl.when(c == ch)
-                    def _():
-                        slot = (shard % 2) * WAYS + c
-                        pltpu.make_async_copy(gbuf.at[slot], grads.at[seq], g_recv).start()
-
-                    @pl.when(c != ch)
-                    def _():
-                        grad_copy(shard, c).start()
-
-                return 0
-
-            lax.fori_loop(0, WAYS, one, 0)
+            pltpu.make_async_copy(gbuf.at[i], grads.at[seq], g_recv).start()
+
+        @pl.when(jnp.logical_not(is_self(i)))
+        def _():
+            grad_copy(2 * ch + i // WAYS, i % WAYS).start()
+
+        return 0
 
     weight_in.wait()
     block = count * WAYS
@@ -366,8 +384,13 @@
     )
     gbuf[...] = mul(pick, graw[...]).astype(BF16).reshape(2 * WAYS, ROWS, CHUNK)
 
+    hello_wait(0)
+    hello_round(1)
     done = [project(0, 0)]
-    give_grads(0, 0)
+    hello_wait(1)
+    hello_round(2)
+    hello_wait(2)
+    hello_round(3)
 
     def follow(dx, dz):
         done.append(project(dx, dz))
@@ -381,74 +404,121 @@
                 tables_of(len(prepared), cols, bands, tables)
                 prepared.append(0)
 
-    for v in range(2):
-        near = ((-1, 0), (1, 0)) if v == 0 else ((0, -1), (0, 1))
-        arrive(v, "P1+")
-        send(v, "P2+")
-        send(v, "Q1+1")
-        send(v, "Q1-1")
-        give_grads(*near[0])
-        arrive(v, "P1-")
-        send(v, "P2-")
-        send(v, "Q1+2")
-        send(v, "Q1-2")
-        give_grads(*near[1])
+    hello_wait(3)
+    lax.fori_loop(0, SHARDS, give_grads, 0)
+    arrive(0, "P1+")
+    send(0, "P2+")
+    send(0, "Q1+1")
+    send(0, "Q1-1")
     pltpu.make_async_copy(packed, params, p_recv).wait()
-    for v in range(2):
-        arrive(v, "Q1+0")
-        send(v, "Q2+0")
-        arrive(v, "Q1-0")
-        send(v, "Q2-0")
+    pltpu.make_async_copy(gain_in, gain_got, k_recv).wait()
     offset = (seq % 2) * block + ch * count
-    select_params(count, offset, params, cols, rows, gains)
-    for v in range(2):
-        arrive(v, "P2+")
-        send(v, "Q1+3a")
-        send(v, "Q1-3a")
-        arrive(v, "P2-")
-        send(v, "Q1+3b")
-        send(v, "Q1-3b")
-        give_grads(*((2, 0) if v == 0 else (0, 2)))
-    for dx, dz in ((-1, 0), (1, 0), (0, -1), (0, 1)):
-        follow(dx, dz)
-    prepare(2)
-    for j in (1, 2):
-        for v in range(2):
-            arrive(v, f"Q1+{j}")
-            send(v, f"Q2+{j}")
-            arrive(v, f"Q1-{j}")
-            send(v, f"Q2-{j}")
-        give_grads(-1 if j == 1 else 1, -1)
-        give_grads(-1 if j == 1 else 1, 1)
-        prepare(2)
-    for dx, dz in ((-1, -1), (-1, 1), (1, -1), (1, 1)):
-        follow(dx, dz)
-        prepare(1)
-    for v in range(2):
-        arrive(v, "Q1+3a")
-        send(v, "Q2+3")
-        arrive(v, "Q1-3b")
-        send(v, "Q2-3")
-        for side in (-1, 1):
-            give_grads(*((2, side) if v == 0 else (side, 2)))
-    for v in range(2):
-        arrive(v, "Q1+3b")
-        arrive(v, "Q1-3a")
-        arrive(v, "Q2+0")
-        arrive(v, "Q2-0")
-    for dx, dz in ((2, 0), (0, 2)):
-        follow(dx, dz)
-        prepare(1)
-    for v in range(2):
-        for j in (1, 2):
-            arrive(v, f"Q2+{j}")
-            arrive(v, f"Q2-{j}")
-    for dx, dz in ((2, -1), (2, 1), (-1, 2), (1, 2)):
-        follow(dx, dz)
-    for v in range(2):
-        arrive(v, "Q2+3")
-        arrive(v, "Q2-3")
-    give_grads(2, 2)
+    select_params(count, offset, params, gain_got, cols, rows, gains)
+    arrive(0, "P1-")
+    send(0, "P2-")
+    send(0, "Q1+2")
+    send(0, "Q1-2")
+    prepare(1)
+    arrive(1, "P1+")
+    send(1, "P2+")
+    send(1, "Q1+1")
+    send(1, "Q1-1")
+    prepare(1)
+    arrive(1, "P1-")
+    send(1, "P2-")
+    send(1, "Q1+2")
+    send(1, "Q1-2")
+    prepare(1)
+    arrive(0, "Q1+0")
+    send(0, "Q2+0")
+    follow(0, -1)
+    prepare(1)
+    arrive(0, "Q1-0")
+    send(0, "Q2-0")
+    follow(0, 1)
+    prepare(1)
+    arrive(1, "Q1+0")
+    send(1, "Q2+0")
+    follow(-1, 0)
+    prepare(1)
+    arrive(1, "Q1-0")
+    send(1, "Q2-0")
+    follow(1, 0)
+    prepare(1)
+    arrive(0, "P2+")
+    send(0, "Q1+3a")
+    send(0, "Q1-3a")
+    prepare(1)
+    arrive(0, "P2-")
+    send(0, "Q1+3b")
+    send(0, "Q1-3b")
+    arrive(0, "Q1+1")
+    arrive(0, "Q1-1")
+    arrive(1, "Q1+1")
+    arrive(1, "Q1-1")
+    arrive(0, "Q1+2")
+    arrive(0, "Q1-2")
+    follow(-1, -1)
+    follow(1, -1)
+    prepare(1)
+    arrive(1, "P2+")
+    send(1, "Q1+3a")
+    send(1, "Q1-3a")
+    prepare(1)
+    arrive(1, "P2-")
+    send(1, "Q1+3b")
+    send(1, "Q1-3b")
+    send(0, "Q2+1")
+    send(0, "Q2-1")
+    send(1, "Q2+1")
+    send(1, "Q2-1")
+    send(0, "Q2+2")
+    send(0, "Q2-2")
+    prepare(1)
+    arrive(1, "Q1+2")
+    send(1, "Q2+2")
+    follow(-1, 1)
+    prepare(1)
+    arrive(1, "Q1-2")
+    send(1, "Q2-2")
+    arrive(1, "Q2+0")
+    arrive(1, "Q2-0")
+    arrive(0, "Q2+0")
+    arrive(0, "Q2-0")
+    follow(1, 1)
+    follow(2, 0)
+    follow(0, 2)
+    prepare(1)
+    arrive(0, "Q1+3a")
+    send(0, "Q2+3")
+    arrive(0, "Q1-3a")
+    arrive(1, "Q1+3a")
+    prepare(1)
+    arrive(0, "Q1-3b")
+    send(0, "Q2-3")
+    send(1, "Q2+3")
+    arrive(1, "Q1-3a")
+    arrive(0, "Q1+3b")
+    prepare(1)
+    arrive(1, "Q1-3b")
+    send(1, "Q2-3")
+    arrive(1, "Q1+3b")
+    arrive(0, "Q2+1")
+    arrive(0, "Q2-1")
+    follow(-1, 2)
+    arrive(1, "Q2+1")
+    arrive(1, "Q2-1")
+    follow(2, -1)
+    arrive(0, "Q2+2")
+    arrive(0, "Q2-2")
+    follow(1, 2)
+    arrive(1, "Q2+2")
+    arrive(1, "Q2-2")
+    follow(2, 1)
+    arrive(0, "Q2+3")
+    arrive(0, "Q2-3")
+    arrive(1, "Q2+3")
+    arrive(1, "Q2-3")
     follow(2, 2)
     deliver(done[-1])
     prepare(count)
@@ -462,13 +532,14 @@
     left, right = pl.ds(0, width // 2), pl.ds(width // 2, width // 2)
     whole = pl.ds(0, width)
     tiles = [pl.ds(0, 16), pl.ds(16, 16), pl.ds(32, TRIO - 32)]
+    straight = (False, False, True)
 
     def owner(step, other):
         return ring(y, step) * 2 + (1 - core if other else core)
 
-    def group_copy(t, n, slot, target, lanes):
+    def group_copy(t, n, slot, target, lanes, own):
         return pltpu.make_async_remote_copy(
-            src_ref=full.at[slot, tiles[t], lanes],
+            src_ref=mine.at[tiles[t], lanes] if own else full.at[slot, tiles[t], lanes],
             dst_ref=full.at[slot, tiles[t], lanes],
             send_sem=a_send.at[t, n],
             recv_sem=a_recv.at[t, n],
@@ -476,56 +547,56 @@
             device_id_type=MESH,
         )
 
-    kinds = [
-        (0, 1, False, whole),
-        (0, -1, False, whole),
-        (0, 0, True, whole),
-        (1, 1, False, left),
-        (-1, -1, False, right),
-        (1, 0, True, whole),
-        (-1, 0, True, whole),
-        (2, 0, True, left),
-        (2, 0, True, right),
-    ]
+    relayed = {
+        0: (0, 1, False, whole),
+        1: (0, -1, False, whole),
+        2: (0, 0, True, whole),
+        3: (1, 1, False, left),
+        4: (-1, -1, False, right),
+        5: (1, 0, True, whole),
+        6: (-1, 0, True, whole),
+        7: (2, 0, True, left),
+        8: (2, 0, True, right),
+    }
+    direct = {n: relayed[n] for n in (0, 1, 2, 5, 6)}
+    direct[3] = (0, 2, False, whole)
+    direct[7] = (2, 0, True, whole)
+    kinds = [direct if straight[t] else relayed for t in range(3)]
 
     def going(t, n):
-        back, step, other, lanes = kinds[n]
-        return group_copy(t, n, owner(-back, False), owner(step, other), lanes)
+        back, step, other, lanes = kinds[t][n]
+        return group_copy(t, n, owner(-back, False), owner(step, other), lanes, back == 0)
 
     def coming(t, n):
-        back, step, other, lanes = kinds[n]
-        return group_copy(t, n, owner(-back - step, other), owner(step, other), lanes)
+        back, step, other, lanes = kinds[t][n]
+        return group_copy(t, n, owner(-back - step, other), owner(step, other), lanes, False)
+
+    def own_copy(t):
+        return pltpu.make_async_copy(
+            mine.at[tiles[t]], full.at[ch, tiles[t]], store_sem.at[t]
+        )
 
     def begin(t):
-        for n in (0, 1, 2):
+        for n in (3, 0, 1, 2) if straight[t] else (0, 1, 2):
             going(t, n).start()
+        own_copy(t).start()
 
     def relay(t):
         coming(t, 0).wait_recv()
-        going(t, 3).start()
+        if not straight[t]:
+            going(t, 3).start()
         going(t, 5).start()
         coming(t, 1).wait_recv()
-        going(t, 4).start()
+        if not straight[t]:
+            going(t, 4).start()
         going(t, 6).start()
 
     def relay_far(t):
         coming(t, 3).wait_recv()
         going(t, 7).start()
-        coming(t, 4).wait_recv()
-        going(t, 8).start()
-
-    mine = full.at[ch]
-    groups = [range(0, 6), range(6, 11), range(11, count)]
-    edges = [(0, 16), (16, 32), (32, TRIO)]
-    for t in range(3):
-        mix_channels(
-            groups[t], rows, gains, bands, tables, projf, projr, gradf, small, skips, outs
-        )
-        pack(outs, mine, *edges[t])
-        begin(t)
-        if t > 0:
-            relay(t - 1)
-    finish_small(count, small, skips)
+        if not straight[t]:
+            coming(t, 4).wait_recv()
+            going(t, 8).start()
 
     def small_copy(i):
         return pltpu.make_async_remote_copy(
@@ -551,64 +622,33 @@
 
         return 0
 
+    groups = [range(0, 6), range(6, 11), range(11, count)]
+    edges = [(0, 16), (16, 32), (32, TRIO)]
+    for t in range(3):
+        mix_channels(
+            groups[t], rows, gains, bands, tables, projf, projr, gradf, small, skips, outs
+        )
+        pack(outs, mine, *edges[t])
+        begin(t)
+    finish_small(count, small, skips)
+    lax.fori_loop(0, SHARDS, start_small, 0)
+    relay(0)
+    relay(1)
     relay_far(0)
-    lax.fori_loop(0, SHARDS, start_small, 0)
+    relay(2)
     relay_far(1)
-    relay(2)
     relay_far(2)
 
-    pltpu.make_async_copy(shared, shared, s_recv).wait()
-    pick = chosen(
-        (2 * WAYS * ROWS, 2 * block),
-        lambda r, c: (r // ROWS == c // count) & (r % ROWS == c % count),
-        F32,
-    )
-    turned = exact(shared[...].reshape(2 * WAYS * ROWS, CHUNK), pick, TN)
-    moment = turned[STATE : 2 * STATE] + turned[2 * STATE : 3 * STATE]
-    residue_out[...] = turned[0:STATE]
-    rate_out[...] = -packed[STATE : 2 * STATE] * jnp.exp(packed[0:STATE]) * moment
-    skip_out[...] = turned[3 * STATE : 3 * STATE + 1]
-
-    for t in range(3):
-        for n in (2, 5, 6, 7, 8):
-            coming(t, n).wait_recv()
-
-    tile = 256
-    gathered = full[...].reshape(WAYS * TRIO, width)
-    sides = []
-    for g in range(3):
-        pick = chosen(
-            (block, WAYS * TRIO),
-            lambda r, c: (c % TRIO == 3 * (r % count) + g) & (c // TRIO == r // count),
-        )
-        sides.append(mul(pick, gathered).astype(BF16))
-    for g in range(3):
-        ordered_grads[g] = sides[g]
-
-    def weight_columns(n, _):
-        lanes = pl.ds(pl.multiple_of(n * tile, tile), tile)
-        right_side = every[:, :, lanes].reshape(width, tile)
-        for g in range(3):
-            wgrad[g, :, lanes] = mul(ordered_grads[g], right_side)
-        return 0
-
-    lax.fori_loop(0, every.shape[2] // tile, weight_columns, 0)
-
-    for t in range(3):
-        for n in range(9):
-            going(t, n).wait_send()
     for v in range(2):
         for name, _ in names:
             feature_copy(v, name, False).wait_send()
     for i in range(1, WAYS):
         pltpu.make_async_copy(parts.at[0], parts.at[i], r_send.at[i]).wait()
 
-    def end_small(i, _):
-        shard = 2 * ch + i // WAYS
-
-        @pl.when(jnp.logical_not(jnp.logical_and(shard == seq, i % WAYS == ch)))
+    def end_sends(i, _):
+        @pl.when(jnp.logical_not(is_self(i)))
         def _():
-            grad_copy(shard, i % WAYS).wait_send()
+            grad_copy(2 * ch + i // WAYS, i % WAYS).wait_send()
 
         @pl.when(jnp.logical_not(small_self(i)))
         def _():
@@ -616,12 +656,52 @@
 
         return 0
 
-    lax.fori_loop(0, SHARDS, end_small, 0)
+    lax.fori_loop(0, SHARDS, end_sends, 0)
 
     @pl.when(at_home)
     def _():
         for i in range(1, WAYS):
             param_copy(i).wait_send()
+            gain_copy(i).wait_send()
+
+    for t in range(3):
+        own_copy(t).wait()
+        for n in kinds[t]:
+            going(t, n).wait_send()
+            if n in (2, 5, 6, 7, 8):
+                coming(t, n).wait_recv()
+    pltpu.make_async_copy(shared, shared, s_recv).wait()
+
+
+def finish(
+    count, features, full, shared, packed, wgrad, residue_out, rate_out, skip_out, rows
+):
+    block = count * WAYS
+    tokens = full.shape[2]
+    width = wgrad.shape[2]
+    lanes = pl.ds(pl.multiple_of(pl.program_id(0) * width, width), width)
+    right_side = features[:, :, lanes].reshape(tokens, width)
+    product = mul(full[...].reshape(WAYS * TRIO, tokens), right_side)
+    for part in range(rows.shape[0]):
+        lanes = pl.ds(part * CHUNK, CHUNK)
+        rows[part] = product[:, part * CHUNK : (part + 1) * CHUNK]
+        for owner in range(WAYS):
+            for g in range(3):
+                own = rows[part, pl.ds(owner * TRIO + g, count, stride=3), :]
+                wgrad[g, owner * count : (owner + 1) * count, lanes] = own
+
+    @pl.when(pl.program_id(0) == 0)
+    def _():
+        pick = chosen(
+            (2 * WAYS * ROWS, 2 * block),
+            lambda r, c: (r // ROWS == c // count) & (r % ROWS == c % count),
+            F32,
+        )
+        turned = exact(shared[...].reshape(2 * WAYS * ROWS, CHUNK), pick, TN)
+        moment = turned[STATE : 2 * STATE] + turned[2 * STATE : 3 * STATE]
+        residue_out[...] = turned[0:STATE]
+        rate_out[...] = -packed[STATE:] * jnp.exp(packed[0:STATE]) * moment
+        skip_out[...] = turned[3 * STATE : 3 * STATE + 1]
 
 
 def local(features, qkv_weight, grad_out, residues, log_rates, skip_gain):
@@ -630,28 +710,31 @@
     count = block // WAYS
     held, order = residues.shape
     weight = qkv_weight.transpose(1, 0, 2)
-    gain = jnp.broadcast_to(skip_gain[None], (8, held))
     anywhere = pl.BlockSpec(memory_space=pl.ANY)
     vmem = pl.BlockSpec(memory_space=pltpu.VMEM)
     dma = pltpu.SemaphoreType.DMA
     tokens = SHARDS * CHUNK
-    weight_grad, residue_grad, rate_grad, skip_grad = pl.pallas_call(
+    operands = [
+        pltpu.with_memory_space_constraint(array, pltpu.MemorySpace.HBM)
+        for array in (
+            features, weight, grad_out, log_rates.T, residues.T, skip_gain.reshape(1, held)
+        )
+    ]
+    every, full, shared, packed = pl.pallas_call(
         functools.partial(kernel, count),
         out_shape=(
-            jax.ShapeDtypeStruct((3, block, width), F32),
-            jax.ShapeDtypeStruct((order, held), F32),
-            jax.ShapeDtypeStruct((order, held), F32),
-            jax.ShapeDtypeStruct((1, held), F32),
+            jax.ShapeDtypeStruct((SHARDS, CHUNK, width), BF16),
+            jax.ShapeDtypeStruct((WAYS, TRIO, tokens), BF16),
+            jax.ShapeDtypeStruct((2 * WAYS, ROWS, CHUNK), F32),
+            jax.ShapeDtypeStruct((PARAM_ROWS, held), F32),
         ),
         in_specs=[anywhere] * 6,
         out_specs=(vmem,) * 4,
         scratch_shapes=[
-            pltpu.VMEM((SHARDS, CHUNK, width), BF16),
             pltpu.VMEM((3, block, width), BF16),
             pltpu.VMEM((WAYS * TRIO, width), BF16),
             pltpu.VMEM((held, CHUNK), BF16),
             pltpu.VMEM((2 * WAYS, ROWS, CHUNK), BF16),
-            pltpu.VMEM((PARAM_ROWS, held), F32),
             pltpu.VMEM((SHARDS, WAYS, TRIO, CHUNK), BF16),
             pltpu.VMEM((WAYS, SHARDS, TRIO, CHUNK), BF16),
             pltpu.VMEM((SHARDS, ROWS, CHUNK), BF16),
@@ -667,9 +750,9 @@
             pltpu.VMEM((SHARDS, TRIO, CHUNK), F32),
             pltpu.VMEM((ROWS, CHUNK), F32),
             pltpu.VMEM((ROWS, CHUNK), F32),
-            pltpu.VMEM((2 * WAYS, ROWS, CHUNK), F32),
-            pltpu.VMEM((WAYS, TRIO, tokens), BF16),
-            pltpu.VMEM((3, block, tokens), BF16),
+            pltpu.VMEM((1, held), F32),
+            pltpu.VMEM((1, held), F32),
+            pltpu.VMEM((TRIO, tokens), BF16),
             dma((6,)),
             dma((2, 22)),
             dma((2, 22)),
@@ -683,11 +766,44 @@
             dma((3, 9)),
             dma((SHARDS,)),
             dma,
+            pltpu.SemaphoreType.REGULAR((4,)),
+            dma((WAYS,)),
+            dma,
+            dma((3,)),
         ],
         compiler_params=pltpu.CompilerParams(
-            collective_id=0, has_side_effects=True, vmem_limit_bytes=48 * 2**20
+            collective_id=0, has_side_effects=True, vmem_limit_bytes=24 * 2**20
         ),
-    )(features, weight, grad_out, log_rates.T, residues.T, gain)
+    )(*operands)
+    columns = 512
+
+    def same(*shape):
+        return pl.BlockSpec(shape, lambda n: (0,) * len(shape))
+
+    weight_grad, residue_grad, rate_grad, skip_grad = pl.pallas_call(
+        functools.partial(finish, count),
+        grid=(width // columns,),
+        out_shape=(
+            jax.ShapeDtypeStruct((3, block, width), F32),
+            jax.ShapeDtypeStruct((order, held), F32),
+            jax.ShapeDtypeStruct((order, held), F32),
+            jax.ShapeDtypeStruct((1, held), F32),
+        ),
+        in_specs=[
+            vmem,
+            vmem,
+            vmem,
+            vmem,
+        ],
+        out_specs=(
+            pl.BlockSpec((3, block, columns), lambda n: (0, 0, n)),
+            same(order, held),
+            same(order, held),
+            same(1, held),
+        ),
+        scratch_shapes=[pltpu.VMEM((columns // CHUNK, WAYS * TRIO, CHUNK), F32)],
+        compiler_params=pltpu.CompilerParams(vmem_limit_bytes=24 * 2**20),
+    )(every, full, shared, packed)
     return weight_grad.transpose(1, 0, 2), residue_grad.T, rate_grad.T, skip_grad.reshape(held)
 
 

time: 70 us -> 56.7 us (0.81); the launches traced: 68.9 us -> 56.6 us
  local copies, waits for them, and re-layouts: 7.77 us -> 0 us
  Pallas kernels: 60.5 us -> 56 us
    pallas_call x1, Pallas kernels: 60.5 us -> 52.9 us  [local(): pl.pallas_call(functools.partial(kernel, count), out_shape=(jax.ShapeDtyp...]
    unnamed x14 -> x0, local copies, waits for them, and re-layouts: 7.09 us -> none
    pallas_call x0 -> x1, Pallas kernels: none -> 3.05 us  [local(): pl.pallas_call(functools.partial(finish, count), grid=(width // columns,)...]
where the time goes in v4:
time: 56.7 us; the launch traced here: 56.6 us
  Pallas kernels  56 us (99%)
  between operations  0.64 us (1%)
    pallas_call x1, Pallas kernels, local(): pl.pallas_call(functools.partial(kernel, count), out_shape=(jax.ShapeDtyp...  52.9 us
    pallas_call x1, Pallas kernels, local(): pl.pallas_call(functools.partial(finish, count), grid=(width // columns,)...  3.05 us

profile of v4, /device:TPU:1, one launch (start us, length us, event | category | flops | bytes accessed | tf_op | source)
XLA Modules:
  0.0 56.6 jit_solution(15922640870729656781)
XLA Ops:
  0.6 52.9 %shard_map.93 = (bf16[16,128,1024]{2,1,0:T(8,128)(2,1)S(1)}, bf16[8,40,2048]{2,1,0:T(8,128)(2,1)S(1)}, f32[16,16,128]{2,1,0:T(8,128)S(1)}, f32[32,208]{1,0:T(8,128)S(1)}) custom-call(bf16[128,1024]{1,0:T(8,128)(2,1)} %feat.1, bf16[3,104,1024]{2,1,0:T(8,128)(2,1)} %bitcast.8, bf16[208,128]{1,0:T(8,128)(2,1)} %gout.1, f32[16,208]{1,0:T(8,128)} %bitcast.9, ...), custom_call_target="tpu_custom_call" | custom-call | tf_op jit(solution)/shard_map/pallas_call | solution.py:723
  53.6 3.0 %shard_map.94 = (f32[3,104,1024]{2,1,0:T(8,128)}, f32[16,208]{1,0:T(8,128)}, f32[16,208]{1,0:T(8,128)}, f32[1,208]{1,0:T(1,128)}) custom-call(bf16[16,128,1024]{2,1,0:T(8,128)(2,1)S(1)} %get-tuple-element.12.features, bf16[8,40,2048]{2,1,0:T(8,128)(2,1)S(1)} %get-tuple-element.13.full, f32[16,16,128]{2,1,0:T(8,128)S(1)} %get-tuple-element.14.shared, ...), custom_call_target="tpu_custom_call" | custom-call | tf_op jit(solution)/shard_map/pallas_call | solution.py:783

commit v5 on v4

--- a/solution.py
+++ b/solution.py
@@ -15,6 +15,7 @@
 ROWS = 16
 TRIO = 40
 STATE = 16
+LATE = 5
 MESH = pl.DeviceIdType.MESH
 PARAM_ROWS = 2 * STATE
 
@@ -39,10 +40,9 @@
     return rule(iota(shape, 0), iota(shape, 1)).astype(kind)
 
 
-def sum_partials(parts, grads, projf, projr, gradf):
+def sum_partials(shards, parts, grads, projf, projr, gradf):
     flip = chosen((CHUNK, CHUNK), lambda r, c: r + c == CHUNK - 1)
-
-    def body(k, _):
+    for k in shards:
         total = parts[0, k].astype(F32)
         for way in range(1, WAYS):
             total = total + parts[way, k].astype(F32)
@@ -50,9 +50,6 @@
         projf[k] = rounded.astype(F32)
         projr[k] = mul(rounded, flip)
         gradf[k] = grads[k].astype(F32)
-        return 0
-
-    lax.fori_loop(0, SHARDS, body, 0, unroll=4)
 
 
 def carry(values, step, lagged, reverse):
@@ -162,18 +159,21 @@
         mine[first:last, k * CHUNK : (k + 1) * CHUNK] = outs[k, first:last].astype(BF16)
 
 
-def finish_small(count, small, skips):
+def finish_small(count, small, skips, tight):
     lane = iota((ROWS, CHUNK), 1)
     row = iota((ROWS, CHUNK), 0)
     summed = jnp.sum(skips[...], axis=1, keepdims=True)
     filled = jnp.where(lane == 3 * STATE, summed, small[...])
-    small[...] = jnp.where(row < count, filled, 0.0)
+    filled = jnp.where(row < count, filled, 0.0)
+    half = ROWS // 2
+    upper = pltpu.roll(filled[half:], CHUNK // 2, 1)
+    tight[...] = jnp.where(lane[:half] < CHUNK // 2, filled[:half], upper)
 
 
 def kernel(
     count, feat, weight, gout, rates_t, residues_t, gain, every, full, shared, packed,
     wraw, wbuf, graw, gbuf, partial, parts, grads, params, cols, rows, gains, bands,
-    tables, projf, projr, gradf, outs, small, skips, gain_in, gain_got, mine,
+    tables, projf, projr, gradf, outs, small, skips, gain_in, gain_got, mine, tight,
     local_sem, f_send, f_recv, r_send, r_recv, g_send, g_recv, p_send, p_recv, a_send, a_recv,
     s_send, s_recv, hello, k_send, k_recv, store_sem,
 ):
@@ -277,13 +277,13 @@
     def hello_wait(n):
         pl.semaphore_wait(hello.at[n], 4)
 
-    def owner_copy(shard, i):
+    def owner_copy(shard, i, batch):
         target = (ch + i) % WAYS
         return pltpu.make_async_remote_copy(
             src_ref=partial.at[shard, target],
             dst_ref=parts.at[i, shard],
-            send_sem=r_send.at[i],
-            recv_sem=r_recv.at[i],
+            send_sem=r_send.at[batch, i],
+            recv_sem=r_recv.at[batch, i],
             device_id={"ch": target},
             device_id_type=MESH,
         )
@@ -298,9 +298,15 @@
         parts[0, shard] = partial[shard, ch]
         return shard
 
-    def deliver(shard):
+    def deliver(at):
         for i in range(1, WAYS):
-            owner_copy(shard, i).start()
+            owner_copy(done[at], i, 0 if at < SHARDS - LATE else 1).start()
+
+    def await_batch(batch, sems):
+        size = LATE if batch else SHARDS - LATE
+        for i in range(1, WAYS):
+            block_of = parts.at[i, pl.ds(0, size)]
+            pltpu.make_async_copy(block_of, block_of, sems.at[batch, i]).wait()
 
     feat_in.wait()
     for v in range(2):
@@ -394,7 +400,7 @@
 
     def follow(dx, dz):
         done.append(project(dx, dz))
-        deliver(done[-2])
+        deliver(len(done) - 2)
 
     prepared = []
 
@@ -405,7 +411,6 @@
                 prepared.append(0)
 
     hello_wait(3)
-    lax.fori_loop(0, SHARDS, give_grads, 0)
     arrive(0, "P1+")
     send(0, "P2+")
     send(0, "Q1+1")
@@ -502,6 +507,7 @@
     prepare(1)
     arrive(1, "Q1-3b")
     send(1, "Q2-3")
+    lax.fori_loop(0, SHARDS, give_grads, 0)
     arrive(1, "Q1+3b")
     arrive(0, "Q2+1")
     arrive(0, "Q2-1")
@@ -520,13 +526,14 @@
     arrive(1, "Q2+3")
     arrive(1, "Q2-3")
     follow(2, 2)
-    deliver(done[-1])
+    deliver(SHARDS - 1)
     prepare(count)
 
     pltpu.make_async_copy(gbuf, grads, g_recv).wait()
-    for i in range(1, WAYS):
-        pltpu.make_async_copy(parts.at[0], parts.at[i], r_recv.at[i]).wait()
-    sum_partials(parts, grads, projf, projr, gradf)
+    await_batch(0, r_recv)
+    sum_partials(done[: SHARDS - LATE], parts, grads, projf, projr, gradf)
+    await_batch(1, r_recv)
+    sum_partials(done[SHARDS - LATE :], parts, grads, projf, projr, gradf)
 
     width = SHARDS * CHUNK
     left, right = pl.ds(0, width // 2), pl.ds(width // 2, width // 2)
@@ -600,7 +607,7 @@
 
     def small_copy(i):
         return pltpu.make_async_remote_copy(
-            src_ref=small,
+            src_ref=tight,
             dst_ref=shared.at[(seq % 2) * WAYS + ch],
             send_sem=s_send.at[i],
             recv_sem=s_recv,
@@ -614,7 +621,7 @@
     def start_small(i, _):
         @pl.when(small_self(i))
         def _():
-            pltpu.make_async_copy(small, shared.at[(seq % 2) * WAYS + ch], s_recv).start()
+            pltpu.make_async_copy(tight, shared.at[(seq % 2) * WAYS + ch], s_recv).start()
 
         @pl.when(jnp.logical_not(small_self(i)))
         def _():
@@ -630,9 +637,9 @@
         )
         pack(outs, mine, *edges[t])
         begin(t)
-    finish_small(count, small, skips)
+    finish_small(count, small, skips, tight)
+    relay(0)
     lax.fori_loop(0, SHARDS, start_small, 0)
-    relay(0)
     relay(1)
     relay_far(0)
     relay(2)
@@ -642,8 +649,8 @@
     for v in range(2):
         for name, _ in names:
             feature_copy(v, name, False).wait_send()
-    for i in range(1, WAYS):
-        pltpu.make_async_copy(parts.at[0], parts.at[i], r_send.at[i]).wait()
+    await_batch(0, r_send)
+    await_batch(1, r_send)
 
     def end_sends(i, _):
         @pl.when(jnp.logical_not(is_self(i)))
@@ -692,12 +699,17 @@
 
     @pl.when(pl.program_id(0) == 0)
     def _():
-        pick = chosen(
-            (2 * WAYS * ROWS, 2 * block),
-            lambda r, c: (r // ROWS == c // count) & (r % ROWS == c % count),
-            F32,
-        )
-        turned = exact(shared[...].reshape(2 * WAYS * ROWS, CHUNK), pick, TN)
+        half = ROWS // 2
+        tiles = shared[...].reshape(2 * WAYS * half, CHUNK)
+        turned = []
+        for first in (0, half):
+            pick = chosen(
+                (2 * WAYS * half, 2 * block),
+                lambda r, c: (r // half == c // count) & (r % half + first == c % count),
+                F32,
+            )
+            turned.append(exact(tiles, pick, TN))
+        turned = turned[0][: CHUNK // 2] + turned[1][CHUNK // 2 :]
         moment = turned[STATE : 2 * STATE] + turned[2 * STATE : 3 * STATE]
         residue_out[...] = turned[0:STATE]
         rate_out[...] = -packed[STATE:] * jnp.exp(packed[0:STATE]) * moment
@@ -725,7 +737,7 @@
         out_shape=(
             jax.ShapeDtypeStruct((SHARDS, CHUNK, width), BF16),
             jax.ShapeDtypeStruct((WAYS, TRIO, tokens), BF16),
-            jax.ShapeDtypeStruct((2 * WAYS, ROWS, CHUNK), F32),
+            jax.ShapeDtypeStruct((2 * WAYS, ROWS // 2, CHUNK), F32),
             jax.ShapeDtypeStruct((PARAM_ROWS, held), F32),
         ),
         in_specs=[anywhere] * 6,
@@ -753,11 +765,12 @@
             pltpu.VMEM((1, held), F32),
             pltpu.VMEM((1, held), F32),
             pltpu.VMEM((TRIO, tokens), BF16),
+            pltpu.VMEM((ROWS // 2, CHUNK), F32),
             dma((6,)),
             dma((2, 22)),
             dma((2, 22)),
-            dma((WAYS,)),
-            dma((WAYS,)),
+            dma((2, WAYS)),
+            dma((2, WAYS)),
             dma((SHARDS,)),
             dma,
             dma((WAYS,)),

time: 56.7 us -> 55.6 us (0.981)
  Pallas kernels: 56 us -> 54.8 us
    pallas_call x1, Pallas kernels: 52.9 us -> 51.6 us  [local(): pl.pallas_call(functools.partial(kernel, count), out_shape=(jax.ShapeDtyp...]
where the time goes in v5:
time: 55.6 us; the launch traced here: 55.5 us
  Pallas kernels  54.8 us (99%)
  between operations  0.64 us (1%)
    pallas_call x1, Pallas kernels, local(): pl.pallas_call(functools.partial(kernel, count), out_shape=(jax.ShapeDtyp...  51.6 us
    pallas_call x1, Pallas kernels, local(): pl.pallas_call(functools.partial(finish, count), grid=(width // columns,)...  3.17 us

profile of v5, /device:TPU:1, one launch (start us, length us, event | category | flops | bytes accessed | tf_op | source)
XLA Modules:
  0.0 55.5 jit_solution(13746450890821846753)
XLA Ops:
  0.6 51.6 %shard_map.93 = (bf16[16,128,1024]{2,1,0:T(8,128)(2,1)S(1)}, bf16[8,40,2048]{2,1,0:T(8,128)(2,1)S(1)}, f32[16,8,128]{2,1,0:T(8,128)S(1)}, f32[32,208]{1,0:T(8,128)S(1)}) custom-call(bf16[128,1024]{1,0:T(8,128)(2,1)} %feat.1, bf16[3,104,1024]{2,1,0:T(8,128)(2,1)} %bitcast.8, bf16[208,128]{1,0:T(8,128)(2,1)} %gout.1, f32[16,208]{1,0:T(8,128)} %bitcast.9, ...), custom_call_target="tpu_custom_call" | custom-call | tf_op jit(solution)/shard_map/pallas_call | solution.py:735
  52.3 3.2 %shard_map.94 = (f32[3,104,1024]{2,1,0:T(8,128)}, f32[16,208]{1,0:T(8,128)}, f32[16,208]{1,0:T(8,128)}, f32[1,208]{1,0:T(1,128)}) custom-call(bf16[16,128,1024]{2,1,0:T(8,128)(2,1)S(1)} %get-tuple-element.12.features, bf16[8,40,2048]{2,1,0:T(8,128)(2,1)S(1)} %get-tuple-element.13.full, f32[16,8,128]{2,1,0:T(8,128)S(1)} %get-tuple-element.14.shared, ...), custom_call_target="tpu_custom_call" | custom-call | tf_op jit(solution)/shard_map/pallas_call | solution.py:796

commit v6 on v5

--- a/solution.py
+++ b/solution.py
@@ -584,7 +584,7 @@
         )
 
     def begin(t):
-        for n in (3, 0, 1, 2) if straight[t] else (0, 1, 2):
+        for n in (0, 1, 3, 2) if straight[t] else (0, 1, 2):
             going(t, n).start()
         own_copy(t).start()
 

time: 55.6 us -> 55.2 us (level)
  no operation moved by 1% of the time
where the time goes in v6:
time: 55.2 us; the launch traced here: 55.1 us
  Pallas kernels  54.5 us (99%)
  between operations  0.64 us (1%)
    pallas_call x1, Pallas kernels, local(): pl.pallas_call(functools.partial(kernel, count), out_shape=(jax.ShapeDtyp...  51.3 us
    pallas_call x1, Pallas kernels, local(): pl.pallas_call(functools.partial(finish, count), grid=(width // columns,)...  3.16 us

profile of v6, /device:TPU:1, one launch (start us, length us, event | category | flops | bytes accessed | tf_op | source)
XLA Modules:
  0.0 55.1 jit_solution(7472931545915040398)
XLA Ops:
  0.6 51.3 %shard_map.93 = (bf16[16,128,1024]{2,1,0:T(8,128)(2,1)S(1)}, bf16[8,40,2048]{2,1,0:T(8,128)(2,1)S(1)}, f32[16,8,128]{2,1,0:T(8,128)S(1)}, f32[32,208]{1,0:T(8,128)S(1)}) custom-call(bf16[128,1024]{1,0:T(8,128)(2,1)} %feat.1, bf16[3,104,1024]{2,1,0:T(8,128)(2,1)} %bitcast.8, bf16[208,128]{1,0:T(8,128)(2,1)} %gout.1, f32[16,208]{1,0:T(8,128)} %bitcast.9, ...), custom_call_target="tpu_custom_call" | custom-call | tf_op jit(solution)/shard_map/pallas_call | solution.py:735
  52.0 3.2 %shard_map.94 = (f32[3,104,1024]{2,1,0:T(8,128)}, f32[16,208]{1,0:T(8,128)}, f32[16,208]{1,0:T(8,128)}, f32[1,208]{1,0:T(1,128)}) custom-call(bf16[16,128,1024]{2,1,0:T(8,128)(2,1)S(1)} %get-tuple-element.12.features, bf16[8,40,2048]{2,1,0:T(8,128)(2,1)S(1)} %get-tuple-element.13.full, f32[16,8,128]{2,1,0:T(8,128)S(1)} %get-tuple-element.14.shared, ...), custom_call_target="tpu_custom_call" | custom-call | tf_op jit(solution)/shard_map/pallas_call | solution.py:796

commit v7 on v6

--- a/solution.py
+++ b/solution.py
@@ -398,9 +398,16 @@
     hello_wait(2)
     hello_round(3)
 
+    delivered = []
+
+    def flush(but=0):
+        while len(delivered) < len(done) - but:
+            deliver(len(delivered))
+            delivered.append(0)
+
     def follow(dx, dz):
         done.append(project(dx, dz))
-        deliver(len(done) - 2)
+        flush(1)
 
     prepared = []
 
@@ -438,18 +445,22 @@
     send(0, "Q2+0")
     follow(0, -1)
     prepare(1)
+    flush()
     arrive(0, "Q1-0")
     send(0, "Q2-0")
     follow(0, 1)
     prepare(1)
+    flush()
     arrive(1, "Q1+0")
     send(1, "Q2+0")
     follow(-1, 0)
     prepare(1)
+    flush()
     arrive(1, "Q1-0")
     send(1, "Q2-0")
     follow(1, 0)
     prepare(1)
+    flush()
     arrive(0, "P2+")
     send(0, "Q1+3a")
     send(0, "Q1-3a")
@@ -466,6 +477,7 @@
     follow(-1, -1)
     follow(1, -1)
     prepare(1)
+    flush()
     arrive(1, "P2+")
     send(1, "Q1+3a")
     send(1, "Q1-3a")
@@ -484,6 +496,7 @@
     send(1, "Q2+2")
     follow(-1, 1)
     prepare(1)
+    flush()
     arrive(1, "Q1-2")
     send(1, "Q2-2")
     arrive(1, "Q2+0")
@@ -494,6 +507,7 @@
     follow(2, 0)
     follow(0, 2)
     prepare(1)
+    flush()
     arrive(0, "Q1+3a")
     send(0, "Q2+3")
     arrive(0, "Q1-3a")
@@ -512,21 +526,25 @@
     arrive(0, "Q2+1")
     arrive(0, "Q2-1")
     follow(-1, 2)
+    flush()
     arrive(1, "Q2+1")
     arrive(1, "Q2-1")
     follow(2, -1)
+    flush()
     arrive(0, "Q2+2")
     arrive(0, "Q2-2")
     follow(1, 2)
+    flush()
     arrive(1, "Q2+2")
     arrive(1, "Q2-2")
     follow(2, 1)
+    flush()
     arrive(0, "Q2+3")
     arrive(0, "Q2-3")
     arrive(1, "Q2+3")
     arrive(1, "Q2-3")
     follow(2, 2)
-    deliver(SHARDS - 1)
+    flush()
     prepare(count)
 
     pltpu.make_async_copy(gbuf, grads, g_recv).wait()

time: 55.2 us -> 54.5 us (0.987)
  Pallas kernels: 54.5 us -> 53.7 us
    pallas_call x1, Pallas kernels: 51.3 us -> 50.6 us  [local(): pl.pallas_call(functools.partial(kernel, count), out_shape=(jax.ShapeDtyp...]
where the time goes in v7:
time: 54.5 us; the launch traced here: 54.4 us
  Pallas kernels  53.7 us (99%)
  between operations  0.64 us (1%)
    pallas_call x1, Pallas kernels, local(): pl.pallas_call(functools.partial(kernel, count), out_shape=(jax.ShapeDtyp...  50.6 us
    pallas_call x1, Pallas kernels, local(): pl.pallas_call(functools.partial(finish, count), grid=(width // columns,)...  3.17 us

profile of v7, /device:TPU:1, one launch (start us, length us, event | category | flops | bytes accessed | tf_op | source)
XLA Modules:
  0.0 54.4 jit_solution(2649702942829189637)
XLA Ops:
  0.6 50.6 %shard_map.93 = (bf16[16,128,1024]{2,1,0:T(8,128)(2,1)S(1)}, bf16[8,40,2048]{2,1,0:T(8,128)(2,1)S(1)}, f32[16,8,128]{2,1,0:T(8,128)S(1)}, f32[32,208]{1,0:T(8,128)S(1)}) custom-call(bf16[128,1024]{1,0:T(8,128)(2,1)} %feat.1, bf16[3,104,1024]{2,1,0:T(8,128)(2,1)} %bitcast.8, bf16[208,128]{1,0:T(8,128)(2,1)} %gout.1, f32[16,208]{1,0:T(8,128)} %bitcast.9, ...), custom_call_target="tpu_custom_call" | custom-call | tf_op jit(solution)/shard_map/pallas_call | solution.py:753
  51.2 3.2 %shard_map.94 = (f32[3,104,1024]{2,1,0:T(8,128)}, f32[16,208]{1,0:T(8,128)}, f32[16,208]{1,0:T(8,128)}, f32[1,208]{1,0:T(1,128)}) custom-call(bf16[16,128,1024]{2,1,0:T(8,128)(2,1)S(1)} %get-tuple-element.12.features, bf16[8,40,2048]{2,1,0:T(8,128)(2,1)S(1)} %get-tuple-element.13.full, f32[16,8,128]{2,1,0:T(8,128)S(1)} %get-tuple-element.14.shared, ...), custom_call_target="tpu_custom_call" | custom-call | tf_op jit(solution)/shard_map/pallas_call | solution.py:814
